TPU v7x, 32 devices: a whole 2x2x4 slice. The times are simulated.
32 devices in a mesh: group: 4 (over x, core), slab: 8 (over z, y).
Axes of the slice: x: 2, y: 2, z: 4, core: 2. Of those that a mesh axis runs over, the one named last changes fastest.
Arguments:
- initial_samples: float32 [96, 64, 4096], P('group', 'slab'), may hold values from -6 to 6
- transport_ratios: float32 [3, 64, 4096], P(None, 'slab'), may hold values from 0.05 to 0.33
- assignment: int32 [96], replicated, may hold values from 0 to 95, each once
- obs_values: float32 [512, 512], P(('group', 'slab')), may hold values from -6 to 6
- obs_error: float32 [512, 512], P(('group', 'slab')), may hold values from 0.25 to 4
- sensor_easting_offset: int32 [512, 512], P(('group', 'slab')), may hold values from 0 to 63
- obs_column: int32 [512, 512], P(('group', 'slab')), may hold values from 0 to 23
- obs_count: int32 [512], P(('group', 'slab')), may hold values from 1 to 512, 131072 in all
Outputs:
- analysis: float32 [96, 64, 4096], P('group', 'slab')
Inputs may be any that keep to these rules, and one draw needn't show every extreme that they name: `assignment`: a permutation of the members. A block's live observations are its first obs_count entries; some block has exactly 512.
All inputs are finite; a program needn't handle non-finite values.
Results may differ from a plain program's by a relative error of at most 0.0003.
Values sent between devices are 32-bit elements; how exact they have to be, the bound alone decides.
No kernel may reach another device: no remote copies, remote signals or barrier semaphores. Data moves between devices by JAX's collectives and lax.ppermute only.
A program may use at most 64 MiB of HBM per device.

v0:
```python
import functools

import jax
import jax.numpy as jnp
from jax import lax
from jax.experimental import pallas as pl
from jax.experimental.pallas import tpu as pltpu
from jax.sharding import PartitionSpec as P

MEMBERS = 96
NZ = 64
STEPS = 6
TILE_WIDTH = 8
HC = 8
OBS = 512
ITERS = 8

LANES = 128
PLANES = 8
SPAN = 16
PACKED = 48
F32 = jnp.float32
BF16 = jnp.bfloat16
AXES = ("group", "slab")
VMEM = pl.BlockSpec(memory_space=pltpu.VMEM)
SMEM = pl.BlockSpec(memory_space=pltpu.SMEM)


def shifted(block, axis, distance):
    devices = range(lax.axis_size(axis))
    route = [((i - distance) % len(devices), i) for i in devices]
    return lax.ppermute(block, axis, route)


def lane_iota(rows=1):
    return lax.broadcasted_iota(jnp.int32, (rows, LANES), 1)


def split(x):
    high = x.astype(BF16)
    low = (x - high.astype(F32)).astype(BF16)
    return high, low


def dot(a, b, transposed=False):
    dims = (((1,), (1 if transposed else 0,)), ((), ()))
    return lax.dot_general(a, b, dims, preferred_element_type=F32)


def dot3(a, b, transposed=False):
    ah, al = a
    bh, bl = b
    return dot(ah, bh, transposed) + (dot(ah, bl, transposed) + dot(al, bh, transposed))


def dot3_deep(a, b):
    ah, al = a
    bh, bl = b
    return dot(jnp.concatenate([ah, al, ah], axis=1), jnp.concatenate([bh, bh, bl], axis=0))


def tile(j):
    return pl.ds(pl.multiple_of(j * LANES, LANES), LANES)


def plane_step(src, dst, slot, rates, plane, tiles):
    lane = lane_iota()
    z_first = (lane % NZ) == 0
    upper = lane >= NZ
    previous = src[slot, :, (tiles - 1) * LANES :]
    octets = src.shape[1] // 8
    for j in range(tiles):
        at = slice(j * LANES, (j + 1) * LANES)
        here = src[slot, :, at]
        upwind = src[slot - 1, :, at]
        below_y = pltpu.roll(jnp.where(upper, previous, here), NZ, 1)
        below_z = jnp.where(z_first, pltpu.roll(here, NZ + 1, 1), pltpu.roll(here, 1, 1))
        cx, cy, cz = (jnp.concatenate([rates[c, plane, :, at]] * octets, axis=0) for c in range(3))
        dst[slot, :, at] = here - cx * (here - upwind) - cy * (here - below_y) - cz * (here - below_z)
        previous = here


def fill(rates, wide):
    for c in range(3):
        for p in range(rates.shape[1]):
            wide[c, p] = jnp.broadcast_to(rates[c, p : p + 1, :], wide.shape[2:])


def first_kernel(x, ratios, skew, edge, a, b, rates):
    tiles = a.shape[2] // LANES
    fill(ratios, rates)

    def unpack(j, carry):
        a[:, :, tile(j)] = jnp.swapaxes(x[:, :, tile(j)], 0, 1)
        return carry

    lax.fori_loop(0, tiles, unpack, 0)
    edge[0] = a[PLANES - 1]

    def two_steps(kk, carry):
        k = 2 * kk + 1

        def up(i, c):
            plane_step(a, b, i, rates, i, tiles)
            return c

        def down(i, c):
            plane_step(b, a, i, rates, i, tiles)
            return c

        lax.fori_loop(k, PLANES, up, 0)
        edge[k] = b[PLANES - 1]
        lax.fori_loop(k + 1, PLANES, down, 0)

        @pl.when(k + 1 < STEPS)
        def _():
            edge[k + 1] = a[PLANES - 1]

        return carry

    lax.fori_loop(0, STEPS // 2, two_steps, 0)
    for p in range(PLANES):
        skew[p] = (a if min(p, STEPS) % 2 == 0 else b)[p]


def exchange_blocks(v):
    block = lane_iota() // SPAN
    for d in (4, 2, 1):
        high = (block // d) % 2 == 1
        out = list(v)
        for i in range(8):
            if (i // d) % 2 == 0:
                out[i] = jnp.where(high, pltpu.roll(v[i + d], SPAN * d, 1), v[i])
                out[i + d] = jnp.where(high, v[i + d], pltpu.roll(v[i], LANES - SPAN * d, 1))
        v = out
    return v


def second_kernel(half, slabs, skew, halo, ratios, zh, keep, send, a, b, rates):
    tiles = a.shape[2] // LANES
    fill(ratios, rates)
    for p in range(STEPS):
        (a if p % 2 == 0 else b)[p + 1] = skew[p]

    def two_steps(kk, carry):
        k = 2 * kk + 1

        def up(i, c):
            plane_step(a, b, i + 1, rates, i, tiles)
            return c

        def down(i, c):
            plane_step(b, a, i + 1, rates, i, tiles)
            return c

        a[0] = halo[k - 1]
        lax.fori_loop(0, k, up, 0)
        b[0] = halo[k]
        lax.fori_loop(0, k + 1, down, 0)
        return carry

    lax.fori_loop(0, STEPS // 2, two_steps, 0)

    lane = lane_iota()
    block = lane // SPAN

    def load(p, j):
        return a[p + 1, :, tile(j)] if p < STEPS else skew[p, :, tile(j)]

    def moved(p, j):
        before = lax.rem(j + (tiles - 1), tiles)
        return pltpu.roll(jnp.where(lane >= LANES - HC, load(p, before), load(p, j)), HC, 1)

    for out, which in ((send, 1 - zh[0]), (keep, zh[0])):

        def chunk(q, carry, out=out, which=which):
            j = lax.div(q, half) * slabs + which * half + lax.rem(q, half)
            groups = exchange_blocks([moved(p, j) for p in range(PLANES)])
            for t in range(8):
                out[q, :, t * LANES : (t + 1) * LANES] = groups[t]
            after = lax.rem(j + 1, tiles)
            last = moved(0, after)
            for p in range(1, PLANES):
                last = jnp.where(block == p, pltpu.roll(moved(p, after), SPAN * p, 1), last)
            out[q, :, 8 * LANES :] = last
            return carry

        lax.fori_loop(0, out.shape[0], chunk, 0)


def map_kernel(half, values, errors, x, column, count, zh, keep, send):
    rows = 4 * half
    row = lax.broadcasted_iota(jnp.int32, (rows, 1), 0)
    second = (row // (2 * half)) % 2
    slab = jnp.where(second == 1, 1 - zh[0], zh[0]) * half + row % half
    is_value = (row // half) % 2 == 1
    cell = lax.broadcasted_iota(jnp.int32, (2 * LANES, OBS), 0)
    slot = lax.broadcasted_iota(jnp.int32, (1, OBS), 1)

    def body(i, carry):
        place = column[i] + TILE_WIDTH * lax.rem(i, 2)
        xs = x[i]
        lanes = (place // SPAN) * LANES + (xs % PLANES) * SPAN + place % SPAN
        hits = jnp.where(cell == lanes, 1.0, 0.0).astype(BF16)
        squared = jnp.where(slot < count[i], 1.0 / (errors[i] * (MEMBERS - 1.0)), 0.0)
        entry = jnp.where(is_value, squared * values[i], squared)
        entry = jnp.where(xs // PLANES == slab, entry, 0.0)
        one, rest = split(entry)
        two, three = split(entry - one.astype(F32))
        sums = dot(jnp.concatenate([one, two, three], axis=0), hits, True)
        total = sums[:rows] + sums[rows : 2 * rows] + sums[2 * rows :]
        keep[i] = total[: 2 * half]
        send[i] = total[2 * half :]
        return carry

    lax.fori_loop(0, values.shape[0], body, 0)


def pack(m):
    lane = lane_iota()
    top = jnp.where(lane < 96, m[64:96], pltpu.roll(m[:32], 96, 1))
    low = jnp.where(lane < 64, m[32:48], pltpu.roll(m[48:64], 64, 1))
    return top, low


def unpack(top, low):
    lane = lane_iota()
    lower = jnp.concatenate(
        [
            jnp.where(lane < 32, pltpu.roll(top, 32, 1), 0.0),
            jnp.where(lane < 64, low, 0.0),
            jnp.where(lane < 64, pltpu.roll(low, 64, 1), 0.0),
            jnp.where(lane < 96, top, 0.0),
            jnp.zeros((32, LANES), F32),
        ],
        axis=0,
    )
    upper = lower.T
    row = lax.broadcasted_iota(jnp.int32, (LANES, LANES), 0)
    col = lax.broadcasted_iota(jnp.int32, (LANES, LANES), 1)
    return jnp.where(row // 32 >= col // 32, lower, upper)


def gram_kernel(half, fields, maps, out, anomaly, high, low, mean):
    groups, members = fields.shape[0] // half, fields.shape[1]
    blocks = maps.shape[0]
    for s in range(half):
        for t in range(fields.shape[2] // LANES):
            at = slice(t * LANES, (t + 1) * LANES)
            f = jnp.concatenate([fields[g * half + s, :, at] for g in range(groups)], axis=0)
            average = jnp.sum(f, axis=0, keepdims=True) / MEMBERS
            f = f - average
            mean[s, :, at] = average
            anomaly[s, :, at] = f
            fh, fl = split(f)
            high[s, :MEMBERS, at] = fh
            low[s, :MEMBERS, at] = fl
            high[s, MEMBERS:, at] = jnp.zeros((LANES - MEMBERS, LANES), BF16)
            low[s, MEMBERS:, at] = jnp.zeros((LANES - MEMBERS, LANES), BF16)

    def pair(i, carry):
        at = pl.ds(pl.multiple_of(i * LANES, LANES), 2 * LANES)
        total = None
        for s in range(half):
            f = anomaly[s, :, at]
            average = mean[s, :, at]
            parts, gammas = [], []
            for e in range(2):
                omega = maps[2 * i + e, s : s + 1, :]
                value = maps[2 * i + e, half + s : half + s + 1, :]
                parts.append(f * omega)
                gammas.append(value - omega * average)
            row = lax.broadcasted_iota(jnp.int32, (8, 2 * LANES), 0)
            extra = jnp.where(row == 0, gammas[0], jnp.where(row == 1, gammas[1], 0.0))
            left = split(jnp.concatenate(parts + [extra], axis=0))
            product = dot3(left, (high[s, :, at], low[s, :, at]), True)
            total = product if total is None else total + product
        for e in range(2):
            top, bottom = pack(total[e * MEMBERS : (e + 1) * MEMBERS])
            base = pl.multiple_of((2 * i + e) * PACKED, 8)
            out[pl.ds(base, 32), :] = top
            out[pl.ds(base + 32, 16), :] = bottom
            out[pl.ds(blocks * PACKED + 2 * i + e, 1), :] = total[2 * MEMBERS + e : 2 * MEMBERS + e + 1]
        return carry

    lax.fori_loop(0, blocks // 2, pair, 0)


def solve_kernel(batch, blocks, mine, other, out, left, right, scale):
    row = lax.broadcasted_iota(jnp.int32, (LANES, LANES), 0)
    col = lax.broadcasted_iota(jnp.int32, (LANES, LANES), 1)
    identity = jnp.where((row == col) & (row < MEMBERS), 1.0, 0.0)
    steps = blocks // batch

    def each(body):
        def several(j, carry):
            for e in range(batch):
                body(j * batch + e)
            return carry

        lax.fori_loop(0, steps, several, 0)

    def start(i):
        base = pl.multiple_of(i * PACKED, 8)
        top = mine[pl.ds(base, 32), :] + other[pl.ds(base, 32), :]
        low = mine[pl.ds(base + 32, 16), :] + other[pl.ds(base + 32, 16), :]
        g = identity + unpack(top, low)
        fro = jnp.sqrt(jnp.sum(jnp.sum(g * g, axis=0, keepdims=True), axis=1, keepdims=True))
        scale[i] = jnp.broadcast_to(fro, (8, LANES))
        left[i] = g * (1.0 / fro)

    def second(i):
        a = left[i]
        middle = 1.5 * identity - 0.5 * a
        left[i] = dot3(split(a), split(middle))
        right[i] = middle

    def iterate(i):
        aa, zz = split(left[i]), split(right[i])
        middle = split(1.5 * identity - 0.5 * dot3(zz, aa))
        left[i] = dot3(aa, middle)
        right[i] = dot3(middle, zz)

    def last(i):
        zz = split(right[i])
        middle = split(1.5 * identity - 0.5 * dot3(zz, split(left[i])))
        right[i] = dot3(middle, zz)

    def finish(i):
        transform = right[i, :MEMBERS] * (1.0 / jnp.sqrt(scale[i, :1]))
        at = pl.ds(blocks * PACKED + i, 1)
        inner = jnp.sum(transform * (mine[at, :] + other[at, :]), axis=1, keepdims=True)
        top, low = pack(transform)
        base = pl.multiple_of(i * PACKED, 8)
        out[pl.ds(base, 32), :] = top
        out[pl.ds(base + 32, 16), :] = low
        out[at, :] = jnp.sum(transform * inner, axis=0, keepdims=True)

    def loop(k, carry):
        each(iterate)
        return carry

    each(start)
    each(second)
    lax.fori_loop(1, ITERS - 1, loop, 0)
    each(last)
    each(finish)


def apply_kernel(half, blocks, fields, weights, assignment, out, result, planar):
    groups, members = fields.shape[0] // half, fields.shape[1]
    lane = lane_iota()
    first = (lane % SPAN) < TILE_WIDTH

    def pair(i, carry):
        sides = []
        for e in range(2):
            base = pl.multiple_of((2 * i + e) * PACKED, 8)
            t = unpack(weights[pl.ds(base, 32), :], weights[pl.ds(base + 32, 16), :])[:MEMBERS]
            sides.append(t + weights[pl.ds(blocks * PACKED + 2 * i + e, 1), :])
        left = split(jnp.concatenate(sides, axis=1))
        filler = jnp.zeros((LANES - MEMBERS, LANES), F32)
        for s in range(half):

            def rows(at):
                return jnp.concatenate([fields[g * half + s, :, at] for g in range(groups)], axis=0)

            x = jnp.where(
                first,
                pltpu.roll(rows(tile(i)), LANES - TILE_WIDTH, 1),
                pltpu.roll(rows(tile(i + 1)), TILE_WIDTH, 1),
            )
            average = jnp.sum(x, axis=0, keepdims=True) / MEMBERS
            x = x - average
            right = jnp.concatenate(
                [jnp.where(first, x, 0.0), filler, jnp.where(first, 0.0, x), filler], axis=0
            )
            result[s, i] = average + dot3(left, split(right))
        return carry

    lax.fori_loop(0, blocks // 2, pair, 0)
    for s in range(half):
        for r in range(MEMBERS // 8):
            at = slice(8 * r, 8 * r + 8)
            planes = exchange_blocks([result[s, i, at, :] for i in range(8)])
            for p in range(PLANES):
                planar[p * MEMBERS + 8 * r : p * MEMBERS + 8 * r + 8, :] = planes[p]

        def hand(n, carry, s=s):
            member = assignment[n]
            g, m = lax.div(member, members), lax.rem(member, members)
            out[g * half + s, m] = planar[pl.ds(n, PLANES, stride=MEMBERS), :]
            return carry

        lax.fori_loop(0, MEMBERS, hand, 0, unroll=8)


def join_kernel(half, mine, other, zh, out):
    for source, which in ((mine, zh[0]), (other, 1 - zh[0])):
        for s in range(half):
            out[:, :, tile(which * half + s)] = source[s]


def call(kernel, outs, scratch, *args, specs=None, cost=None):
    shapes = [jax.ShapeDtypeStruct(s, F32) for s in outs]
    return pl.pallas_call(
        kernel,
        out_shape=shapes if len(shapes) > 1 else shapes[0],
        in_specs=specs or [VMEM] * len(args),
        out_specs=[VMEM] * len(shapes) if len(shapes) > 1 else VMEM,
        scratch_shapes=scratch,
        compiler_params=pltpu.CompilerParams(vmem_limit_bytes=56 * 1024 * 1024),
        cost_estimate=cost,
    )(*args)


def work(flops, moved):
    return pl.CostEstimate(flops=flops, bytes_accessed=moved, transcendentals=0)


def planned(
    initial_samples,
    transport_ratios,
    assignment,
    obs_values,
    obs_error,
    sensor_easting_offset,
    obs_column,
    obs_count,
):
    members, planes, columns = initial_samples.shape
    slabs = lax.axis_size("slab")
    groups = lax.axis_size("group")
    half = slabs // 2
    peers = groups * half
    blocks = obs_values.shape[0]
    width = blocks // 2 * LANES + LANES
    zh = (lax.axis_index("slab") // half).astype(jnp.int32).reshape(1)
    teams = [
        [g * slabs + h * half + i for g in range(groups) for i in range(half)] for h in range(2)
    ]

    def spread(x):
        return lax.all_to_all(
            x, AXES, split_axis=0, concat_axis=0, tiled=True, axis_index_groups=teams
        )

    def partner(x):
        return shifted(x, "slab", half)

    whole = (planes, members, columns)
    wide = [pltpu.VMEM((3, planes, 8, columns), F32)]
    skew, edge = call(
        first_kernel,
        [whole, (STEPS, members, columns)],
        [pltpu.VMEM(whole, F32)] * 2 + wide,
        initial_samples,
        transport_ratios,
        cost=work(10**7, 10**7),
    )
    halo = shifted(edge, "slab", 1)
    map_shape = (blocks, 2 * half, 2 * LANES)
    map_keep, map_send = call(
        functools.partial(map_kernel, half),
        [map_shape, map_shape],
        [],
        *(x[:, None] for x in (obs_values, obs_error, sensor_easting_offset, obs_column)),
        obs_count,
        zh,
        specs=[VMEM] * 4 + [SMEM] * 2,
        cost=work(10**8, 10**6),
    )
    map_recv = partner(map_send)
    payload = (peers, members, width)
    keep, send = call(
        functools.partial(second_kernel, half, slabs),
        [payload, payload],
        [pltpu.VMEM((STEPS + 1, members, columns), F32)] * 2 + wide,
        skew,
        halo,
        transport_ratios,
        zh,
        specs=[VMEM] * 3 + [SMEM],
        cost=work(10**7, 10**7),
    )
    packed = (blocks * PACKED + blocks, LANES)

    def gram(fields, maps):
        return call(
            functools.partial(gram_kernel, half),
            [packed],
            [
                pltpu.VMEM((half, MEMBERS, width), F32),
                pltpu.VMEM((half, LANES, width), BF16),
                pltpu.VMEM((half, LANES, width), BF16),
                pltpu.VMEM((half, 1, width), F32),
            ],
            fields,
            maps,
            cost=work(10**9, 4 * 10**6),
        )

    def apply(fields, weights):
        return call(
            functools.partial(apply_kernel, half, blocks),
            [(peers, members, planes, LANES)],
            [
                pltpu.VMEM((half, blocks // 2, MEMBERS, LANES), F32),
                pltpu.VMEM((PLANES * MEMBERS, LANES), F32),
            ],
            fields,
            weights,
            assignment,
            specs=[VMEM] * 2 + [SMEM],
            cost=work(10**9, 4 * 10**6),
        )

    fields_send = spread(send)
    gram_other = partner(gram(fields_send, map_recv))
    fields_keep = spread(keep)
    gram_mine = gram(fields_keep, map_keep)
    weights = call(
        functools.partial(solve_kernel, 8, blocks),
        [packed],
        [pltpu.VMEM((blocks, LANES, LANES), F32)] * 2 + [pltpu.VMEM((blocks, 8, LANES), F32)],
        gram_mine,
        gram_other,
        cost=work(10**9, 10**6),
    )
    weights_other = partner(weights)
    result_mine = spread(apply(fields_keep, weights))
    result_other = spread(apply(fields_send, weights_other))
    part = pl.BlockSpec((half, members, planes, LANES), lambda g: (g, 0, 0, 0))
    return pl.pallas_call(
        functools.partial(join_kernel, half),
        out_shape=jax.ShapeDtypeStruct((members, planes, columns), F32),
        grid=(groups,),
        in_specs=[part, part, SMEM],
        out_specs=pl.BlockSpec((members, planes, slabs * LANES), lambda g: (0, 0, g)),
    )(result_mine, result_other, zh)


def padded(x, sides, width):
    for axis, dim in sides:
        size, length = (lax.axis_size(axis), x.shape[dim])
        up = [(i, (i + 1) % size) for i in range(size)]
        down = [(j, i) for i, j in up]
        last = lax.slice_in_dim(x, length - width, length, axis=dim)
        first = lax.slice_in_dim(x, 0, width, axis=dim)
        before = lax.ppermute(last, axis, up)
        after = lax.ppermute(first, axis, down)
        x = jnp.concatenate([before, x, after], axis=dim)
    return x


def advance(sample_state, upwind, rates):
    z_position = jnp.arange(sample_state.shape[2]) % NZ
    below_y = jnp.roll(sample_state, NZ, axis=2)
    below_z = jnp.where(
        z_position == 0, jnp.roll(sample_state, 1 - NZ, axis=2), jnp.roll(sample_state, 1, axis=2)
    )
    return (
        sample_state
        - rates[0] * (sample_state - upwind)
        - rates[1] * (sample_state - below_y)
        - rates[2] * (sample_state - below_z)
    )


def general(
    initial_samples,
    transport_ratios,
    assignment,
    obs_values,
    obs_error,
    sensor_easting_offset,
    obs_column,
    obs_count,
):
    hi = lax.Precision.HIGHEST
    local_members, planes, total_columns = initial_samples.shape
    group_count = lax.axis_size("group")
    slab_count = lax.axis_size("slab")
    own_columns = total_columns // (group_count * slab_count)
    state = initial_samples
    for section in range(STEPS):
        edge_plane = shifted(state[:, planes - 1 :], "slab", 1)
        upwind = jnp.concatenate([edge_plane, state[:, : planes - 1]], axis=1)
        state = advance(state, upwind, transport_ratios)
    pieces = lax.all_to_all(state, ("group", "slab"), split_axis=2, concat_axis=0, tiled=True)
    pieces = pieces.reshape(group_count, slab_count, local_members, planes, own_columns)
    vertical_line_positions = jnp.transpose(pieces, (0, 2, 1, 3, 4)).reshape(
        MEMBERS, slab_count * planes, own_columns
    )
    grid_x = vertical_line_positions.shape[1]
    own_blocks = obs_values.shape[0]
    block_start = (TILE_WIDTH * jnp.arange(own_blocks, dtype=jnp.int32))[:, None]
    edge_blocks = (HC + TILE_WIDTH - 1) // TILE_WIDTH
    window_col = block_start - HC + obs_column
    requests = jnp.stack([sensor_easting_offset, obs_column])
    asked = padded(requests, ((("group", "slab"), 1),), edge_blocks)
    left_asked = asked[:, :edge_blocks]
    right_asked = asked[:, edge_blocks + own_blocks :]
    edge_index = jnp.arange(edge_blocks, dtype=jnp.int32)[:, None]
    left_cols = (
        TILE_WIDTH * (own_blocks - edge_blocks + edge_index) - HC + left_asked[1] - own_columns
    )
    right_cols = TILE_WIDTH * edge_index - HC + right_asked[1] + own_columns
    serve_level = jnp.concatenate([left_asked[0], right_asked[0]], axis=0)
    serve_cols = jnp.clip(jnp.concatenate([left_cols, right_cols], axis=0), 0, own_columns - 1)
    flattened = vertical_line_positions.reshape(MEMBERS, grid_x * own_columns)
    serve_pos = (serve_level * own_columns + serve_cols).reshape(-1)
    served = jnp.take(flattened, serve_pos, axis=1).reshape(MEMBERS, 2 * edge_blocks, OBS)
    answered = padded(served, ((("group", "slab"), 1),), edge_blocks)
    from_left = answered[:, :edge_blocks]
    from_right = answered[:, 3 * edge_blocks :]
    filler = jnp.zeros((MEMBERS, own_blocks - edge_blocks, OBS), jnp.float32)
    left_full = jnp.concatenate([from_left, filler], axis=1)
    right_full = jnp.concatenate([filler, from_right], axis=1)
    local_pos = (
        sensor_easting_offset * own_columns + jnp.clip(window_col, 0, own_columns - 1)
    ).reshape(-1)
    local_vals = jnp.take(flattened, local_pos, axis=1).reshape(MEMBERS, own_blocks, OBS)
    modelled_readings = jnp.where(
        window_col[None] < 0,
        left_full,
        jnp.where(window_col[None] >= own_columns, right_full, local_vals),
    )
    slots = jnp.arange(OBS, dtype=jnp.int32)[None, :]
    pred_mean = jnp.mean(modelled_readings, axis=0)
    weight = jnp.where(slots < obs_count[:, None], 1.0 / jnp.sqrt(obs_error * (MEMBERS - 1.0)), 0.0)
    scaled = jnp.transpose((modelled_readings - pred_mean[None]) * weight[None], (1, 0, 2))
    innovation = (obs_values - pred_mean) * weight
    identity = jnp.eye(MEMBERS, dtype=jnp.float32)
    gram = identity[None] + jnp.einsum("bmk,bnk->bmn", scaled, scaled, precision=hi)
    fro_norm = jnp.sqrt(jnp.sum(gram * gram, axis=(1, 2)))
    iterate_a = gram / fro_norm[:, None, None]
    iterate_z = jnp.broadcast_to(identity, gram.shape)
    for iteration in range(ITERS):
        middle = 1.5 * identity[None] - 0.5 * jnp.einsum(
            "bij,bjk->bik", iterate_z, iterate_a, precision=hi
        )
        iterate_a = jnp.einsum("bij,bjk->bik", iterate_a, middle, precision=hi)
        iterate_z = jnp.einsum("bij,bjk->bik", middle, iterate_z, precision=hi)
    transform = iterate_z / jnp.sqrt(fro_norm)[:, None, None]
    projected = jnp.einsum("bmk,bk->bm", scaled, innovation, precision=hi)
    inner_step = jnp.einsum("bmn,bn->bm", transform, projected, precision=hi)
    mean_weights = jnp.einsum("bmn,bn->bm", transform, inner_step, precision=hi)
    weights_all = mean_weights[:, :, None] + transform
    one_hot = (assignment[:, None] == jnp.arange(MEMBERS, dtype=jnp.int32)[None, :]).astype(
        jnp.float32
    )
    ordered = jnp.einsum("bmn,nj->bmj", weights_all, one_hot, precision=hi)
    column_weights = jnp.repeat(ordered, TILE_WIDTH, axis=0)
    column_major = jnp.transpose(vertical_line_positions, (2, 0, 1))
    cell_mean = jnp.mean(column_major, axis=1)
    updated = cell_mean[:, None, :] + jnp.einsum(
        "cmj,cmx->cjx", column_weights, column_major - cell_mean[:, None, :], precision=hi
    )
    analysed = jnp.transpose(updated, (1, 2, 0))
    outgoing = analysed.reshape(group_count, local_members, slab_count, planes, own_columns)
    outgoing = jnp.transpose(outgoing, (0, 2, 1, 3, 4)).reshape(
        group_count * slab_count * local_members, planes, own_columns
    )
    result = lax.all_to_all(outgoing, ("group", "slab"), split_axis=0, concat_axis=2, tiled=True)
    return result


def shards(initial_samples, transport_ratios, assignment, obs_values, *rest):
    members, planes, columns = initial_samples.shape
    blocks = obs_values.shape[0]
    fits = (
        planes == PLANES
        and members % 8 == 0
        and blocks * TILE_WIDTH == LANES
        and lax.axis_size("slab") == 8
        and columns % LANES == 0
    )
    path = planned if fits else general
    return path(initial_samples, transport_ratios, assignment, obs_values, *rest)


def solution(mesh):
    placed = (
        P("group", "slab", None),
        P(None, "slab", None),
        P(),
        P(("group", "slab"), None),
        P(("group", "slab"), None),
        P(("group", "slab"), None),
        P(("group", "slab"), None),
        P(("group", "slab")),
    )
    return jax.shard_map(
        shards, mesh=mesh, in_specs=placed, out_specs=P("group", "slab", None), check_vma=False
    )
```

profile of v0, /device:TPU:0, one launch (start us, length us, event | category | flops | bytes accessed | tf_op | source)
XLA Modules:
  0.0 304.4 jit_solution(2057117702301707657)
XLA Ops:
  0.0 15.8 %shard_map.82 = (f32[8,24,4096]{2,1,0:T(8,128)}, f32[6,24,4096]{2,1,0:T(8,128)}) custom-call(f32[24,8,4096]{2,1,0:T(8,128)} %x.1, f32[3,8,4096]{2,1,0:T(8,128)} %ratios.3), custom_call_target="tpu_custom_call" | custom-call | flops 10000000 | bytes 10000000 | tf_op jit(solution)/shard_map/pallas_call | solution.py:406
  15.8 3.0 collective-permute-start
  18.8 54.5 %collective-permute-done.halo = f32[6,24,4096]{2,1,0:T(8,128)S(1)} collective-permute-done((f32[6,24,4096]{2,1,0:T(8,128)}, f32[6,24,4096]{2,1,0:T(8,128)S(1)}, u32[]{:S(2)}, u32[]{:S(2)}) %collective-permute-start) | collective-permute-done | bytes 2359328 | tf_op jit(solution)/shard_map/ppermute | solution.py:32
  73.3 1.4 copy-done.2
  74.8 23.4 %shard_map.83 = (f32[16,24,1152]{2,1,0:T(8,128)}, f32[16,24,1152]{2,1,0:T(8,128)}) custom-call(f32[8,24,4096]{2,1,0:T(8,128)} %get-tuple-element.11.skew, f32[6,24,4096]{2,1,0:T(8,128)} %copy-done.2, f32[3,8,4096]{2,1,0:T(8,128)} %ratios.3, s32[1]{0:T(128)} %bitcast.zh), custom_call_target="tpu_custom_call" | custom-call | flops 10000000 | bytes 10000000 | tf_op jit(solution)/shard_map/pallas_call | solution.py:406
  98.1 28.0 %all_to_all.20.fields = f32[16,24,1152]{2,1,0:T(8,128)} all-to-all(f32[16,24,1152]{2,1,0:T(8,128)} %get-tuple-element.15), channel_id=1, replica_groups={{0,1,2,3,8,9,10,11,16,17,18,19,24,25,26,27},{4,5,6,7,12,13,14,15,20,21,..., dimensions={0} | all-to-all | bytes 3538944 | tf_op jit(solution)/shard_map/all_to_all | solution.py:444
  126.2 3.9 %all-to-all-start = ((f32[16,24,1152]{2,1,0:T(8,128)}), f32[16,24,1152]{2,1,0:T(8,128)S(1)}, u32[]{:S(2)}, u32[]{:S(2)}) async-start(f32[16,24,1152]{2,1,0:T(8,128)} %get-tuple-element.13), calls=%async_computation | async-start | bytes 3538944 | tf_op jit(solution)/shard_map/all_to_all | solution.py:444
  132.6 5.0 %shard_map.84 = (f32[16,8,256]{2,1,0:T(8,128)}, f32[16,8,256]{2,1,0:T(8,128)}) custom-call(f32[16,1,512]{2,1,0:T(1,128)} %broadcast_in_dim.12.values, f32[16,1,512]{2,1,0:T(1,128)} %broadcast_in_dim.13.errors, s32[16,1,512]{2,1,0:T(1,128)} %broadcast_in_dim.14.x, s32[16,1,512]{2,1,0:T(1,128)} %broadcast_in_dim.15.column, s32[16]{0:T(128)} %count.1, s32[1]{0:T(128)} %bitcast.zh), custom_call_target="tpu_custom_call" | custom-call | flops 100000000 | bytes 1000000 | tf_op jit(solution)/shard_map/pallas_call | solution.py:406
  138.3 15.1 %collective-permute-done.1.maps = f32[16,8,256]{2,1,0:T(8,128)S(1)} collective-permute-done((f32[16,8,256]{2,1,0:T(8,128)}, f32[16,8,256]{2,1,0:T(8,128)S(1)}, u32[]{:S(2)}, u32[]{:S(2)}) %collective-permute-start.1) | collective-permute-done | bytes 131104 | tf_op jit(solution)/shard_map/ppermute | solution.py:32
  154.1 7.3 %shard_map.86 = f32[784,128]{1,0:T(8,128)} custom-call(f32[16,24,1152]{2,1,0:T(8,128)} %all_to_all.20.fields, f32[16,8,256]{2,1,0:T(8,128)} %copy-done.10), custom_call_target="tpu_custom_call" | custom-call | flops 1000000000 | bytes 4000000 | tf_op jit(solution)/shard_map/pallas_call | solution.py:406
  161.3 3.3 %collective-permute-start.2 = (f32[784,128]{1,0:T(8,128)}, f32[784,128]{1,0:T(8,128)S(1)}, u32[]{:S(2)}, u32[]{:S(2)}) collective-permute-start(f32[784,128]{1,0:T(8,128)} %shard_map.86), channel_id=1, source_target_pairs={{4,0},{5,1},{6,2},{7,3},{0,4},{1,5},{2,6},{3,7},{12,8},{13,9},{14,... | collective-permute-start | bytes 1204232 | tf_op jit(solution)/shard_map/ppermute | solution.py:32
  164.6 1.2 copy-done
  165.8 7.3 %shard_map.85.mine = f32[784,128]{1,0:T(8,128)} custom-call(f32[16,24,1152]{2,1,0:T(8,128)} %copy-done, f32[16,8,256]{2,1,0:T(8,128)} %get-tuple-element.14.maps), custom_call_target="tpu_custom_call" | custom-call | flops 1000000000 | bytes 4000000 | tf_op jit(solution)/shard_map/pallas_call | solution.py:406
  173.1 9.6 %collective-permute-done.2.other = f32[784,128]{1,0:T(8,128)S(1)} collective-permute-done((f32[784,128]{1,0:T(8,128)}, f32[784,128]{1,0:T(8,128)S(1)}, u32[]{:S(2)}, u32[]{:S(2)}) %collective-permute-start.2) | collective-permute-done | bytes 401440 | tf_op jit(solution)/shard_map/ppermute | solution.py:32
  182.7 0.7 copy-done.9
  183.5 30.5 %shard_map.87.weights = f32[784,128]{1,0:T(8,128)} custom-call(f32[784,128]{1,0:T(8,128)} %shard_map.85.mine, f32[784,128]{1,0:T(8,128)} %copy-done.9), custom_call_target="tpu_custom_call" | custom-call | flops 1000000000 | bytes 1000000 | tf_op jit(solution)/shard_map/pallas_call | solution.py:406
  214.0 12.5 %shard_map.88 = f32[16,24,8,128]{3,2,1,0:T(8,128)} custom-call(f32[16,24,1152]{2,1,0:T(8,128)} %copy-done, f32[784,128]{1,0:T(8,128)} %shard_map.87.weights, s32[96]{0:T(128)} %assignment.3), custom_call_target="tpu_custom_call" | custom-call | flops 1000000000 | bytes 4000000 | tf_op jit(solution)/shard_map/pallas_call | solution.py:406
  226.5 3.8 %all-to-all-start.2 = ((f32[16,24,8,128]{3,2,1,0:T(8,128)}), f32[16,24,8,128]{3,2,1,0:T(8,128)S(1)}, u32[]{:S(2)}, u32[]{:S(2)}) async-start(f32[16,24,8,128]{3,2,1,0:T(8,128)} %shard_map.88), calls=%async_computation.2 | async-start | bytes 3145728 | tf_op jit(solution)/shard_map/all_to_all | solution.py:444
  230.3 2.4 collective-permute-start.3
  232.7 24.2 %collective-permute-done.3.weights = f32[784,128]{1,0:T(8,128)S(1)} collective-permute-done((f32[784,128]{1,0:T(8,128)S(1)}, f32[784,128]{1,0:T(8,128)S(1)}, u32[]{:S(2)}, u32[]{:S(2)}) %collective-permute-start.3) | collective-permute-done | bytes 401440 | tf_op jit(solution)/shard_map/ppermute | solution.py:32
  257.0 0.8 copy-done.4
  257.7 12.5 %shard_map.89 = f32[16,24,8,128]{3,2,1,0:T(8,128)} custom-call(f32[16,24,1152]{2,1,0:T(8,128)} %all_to_all.20.fields, f32[784,128]{1,0:T(8,128)} %copy-done.4, s32[96]{0:T(128)} %assignment.3), custom_call_target="tpu_custom_call" | custom-call | flops 1000000000 | bytes 4000000 | tf_op jit(solution)/shard_map/pallas_call | solution.py:406
  270.2 29.9 %all_to_all.21.other = f32[16,24,8,128]{3,2,1,0:T(8,128)} all-to-all(f32[16,24,8,128]{3,2,1,0:T(8,128)} %shard_map.89), channel_id=1, replica_groups={{0,1,2,3,8,9,10,11,16,17,18,19,24,25,26,27},{4,5,6,7,12,13,14,15,20,21,..., dimensions={0} | all-to-all | bytes 3145728 | tf_op jit(solution)/shard_map/all_to_all | solution.py:444
  300.1 4.2 %shard_map.90 = f32[24,8,4096]{2,1,0:T(8,128)} custom-call(f32[16,24,8,128]{3,2,1,0:T(8,128)} %copy-done.1, f32[16,24,8,128]{3,2,1,0:T(8,128)} %all_to_all.21.other, s32[1]{0:T(128)} %bitcast.zh), custom_call_target="tpu_custom_call" | custom-call | tf_op jit(solution)/shard_map/pallas_call | solution.py:534
  (25 shorter events, 3.9 us)
Async XLA Ops:
  15.8 57.5 %collective-permute-start = (f32[6,24,4096]{2,1,0:T(8,128)}, f32[6,24,4096]{2,1,0:T(8,128)S(1)}, u32[]{:S(2)}, u32[]{:S(2)}) collective-permute-start(f32[6,24,4096]{2,1,0:T(8,128)} %get-tuple-element.12), channel_id=1, source_target_pairs={{7,0},{0,1},{1,2},{2,3},{3,4},{4,5},{5,6},{6,7},{15,8},{8,9},{9,10... | collective-permute-start | bytes 7077896 | tf_op jit(solution)/shard_map/ppermute | solution.py:32
  73.3 1.4 copy-start.2
  126.2 3.9 %copy-start.5 = (f32[16,512]{1,0:T(8,128)S(1)}, f32[16,512]{1,0:T(8,128)}, u32[]{:S(2)}) copy-start(f32[16,512]{1,0:T(8,128)} %param.11) | copy-start | bytes 98308
  126.2 4.5 %copy-start.6 = (f32[16,512]{1,0:T(8,128)S(1)}, f32[16,512]{1,0:T(8,128)}, u32[]{:S(2)}) copy-start(f32[16,512]{1,0:T(8,128)} %param.12) | copy-start | bytes 98308
  126.2 5.1 %copy-start.7 = (s32[16,512]{1,0:T(8,128)S(1)}, s32[16,512]{1,0:T(8,128)}, u32[]{:S(2)}) copy-start(s32[16,512]{1,0:T(8,128)} %param.13) | copy-start | bytes 98308
  126.2 5.8 %copy-start.8 = (s32[16,512]{1,0:T(8,128)S(1)}, s32[16,512]{1,0:T(8,128)}, u32[]{:S(2)}) copy-start(s32[16,512]{1,0:T(8,128)} %param.14) | copy-start | bytes 98308
  126.2 38.4 %all-to-all-start = ((f32[16,24,1152]{2,1,0:T(8,128)}), f32[16,24,1152]{2,1,0:T(8,128)S(1)}, u32[]{:S(2)}, u32[]{:S(2)}) async-start(f32[16,24,1152]{2,1,0:T(8,128)} %get-tuple-element.13), calls=%async_computation | async-start | bytes 3538944 | tf_op jit(solution)/shard_map/all_to_all | solution.py:444
  137.6 15.8 %collective-permute-start.1 = (f32[16,8,256]{2,1,0:T(8,128)}, f32[16,8,256]{2,1,0:T(8,128)S(1)}, u32[]{:S(2)}, u32[]{:S(2)}) collective-permute-start(f32[16,8,256]{2,1,0:T(8,128)} %get-tuple-element.16), channel_id=1, source_target_pairs={{4,0},{5,1},{6,2},{7,3},{0,4},{1,5},{2,6},{3,7},{12,8},{13,9},{14,... | collective-permute-start | bytes 393224 | tf_op jit(solution)/shard_map/ppermute | solution.py:32
  153.4 0.7 copy-start.10
  161.3 21.4 %collective-permute-start.2 = (f32[784,128]{1,0:T(8,128)}, f32[784,128]{1,0:T(8,128)S(1)}, u32[]{:S(2)}, u32[]{:S(2)}) collective-permute-start(f32[784,128]{1,0:T(8,128)} %shard_map.86), channel_id=1, source_target_pairs={{4,0},{5,1},{6,2},{7,3},{0,4},{1,5},{2,6},{3,7},{12,8},{13,9},{14,... | collective-permute-start | bytes 1204232 | tf_op jit(solution)/shard_map/ppermute | solution.py:32
  164.6 1.2 copy-start
  182.7 0.7 copy-start.9
  226.5 3.9 %copy-start.3 = (f32[784,128]{1,0:T(8,128)S(1)}, f32[784,128]{1,0:T(8,128)}, u32[]{:S(2)}) copy-start(f32[784,128]{1,0:T(8,128)} %shard_map.87.weights) | copy-start | bytes 1204228
  226.5 43.7 %all-to-all-start.2 = ((f32[16,24,8,128]{3,2,1,0:T(8,128)}), f32[16,24,8,128]{3,2,1,0:T(8,128)S(1)}, u32[]{:S(2)}, u32[]{:S(2)}) async-start(f32[16,24,8,128]{3,2,1,0:T(8,128)} %shard_map.88), calls=%async_computation.2 | async-start | bytes 3145728 | tf_op jit(solution)/shard_map/all_to_all | solution.py:444
  230.3 26.7 %collective-permute-start.3 = (f32[784,128]{1,0:T(8,128)S(1)}, f32[784,128]{1,0:T(8,128)S(1)}, u32[]{:S(2)}, u32[]{:S(2)}) collective-permute-start(f32[784,128]{1,0:T(8,128)S(1)} %copy-done.3), channel_id=1, source_target_pairs={{4,0},{5,1},{6,2},{7,3},{0,4},{1,5},{2,6},{3,7},{12,8},{13,9},{14,... | collective-permute-start | bytes 1204232 | tf_op jit(solution)/shard_map/ppermute | solution.py:32
  257.0 0.8 copy-start.4
  270.2 29.9 %copy-start.1 = (f32[16,24,8,128]{3,2,1,0:T(8,128)}, f32[16,24,8,128]{3,2,1,0:T(8,128)S(1)}, u32[]{:S(2)}) copy-start(f32[16,24,8,128]{3,2,1,0:T(8,128)S(1)} %all-to-all-done.2.mine) | copy-start | bytes 4718596
where the time goes:
time: 305 us; the launch traced here: 304 us
  Pallas kernels  119 us (39%)
  waiting for transfers between devices  103 us (34%)
  blocking collectives  58 us (19%)
  starting transfers between devices  17.1 us (6%)
  local copies, waits for them, and re-layouts  7.33 us (2%)
    pallas_call x8, Pallas kernels, call(): pl.pallas_call(kernel, out_shape=shapes if len(shapes) > 1 else shapes[0]...  114 us
    ppermute x4, waiting for transfers between devices, shifted(): return lax.ppermute(block, axis, route)  103 us
    all_to_all x2, blocking collectives, spread(): lax.all_to_all(x, AXES, split_axis=0, concat_axis=0, tiled=True, axis_ind...  58 us
    ppermute x4, starting transfers between devices, shifted(): return lax.ppermute(block, axis, route)  9.36 us
    all_to_all x2, starting transfers between devices, spread(): lax.all_to_all(x, AXES, split_axis=0, concat_axis=0, tiled=True, axis_ind...  7.69 us
  transfers between devices with their start and end apart: 6, of which 4 were waited for; matrix products, arithmetic and copies ran while one was open for 1% of the time, Pallas kernels for 11%

commit v1 on v0

--- a/solution.py
+++ b/solution.py
@@ -6,6 +6,7 @@
 from jax.experimental import pallas as pl
 from jax.experimental.pallas import tpu as pltpu
 from jax.sharding import PartitionSpec as P
+
 
 MEMBERS = 96
 NZ = 64
@@ -19,6 +20,7 @@
 PLANES = 8
 SPAN = 16
 PACKED = 48
+BATCH = 4
 F32 = jnp.float32
 BF16 = jnp.bfloat16
 AXES = ("group", "slab")
@@ -53,12 +55,6 @@
     return dot(ah, bh, transposed) + (dot(ah, bl, transposed) + dot(al, bh, transposed))
 
 
-def dot3_deep(a, b):
-    ah, al = a
-    bh, bl = b
-    return dot(jnp.concatenate([ah, al, ah], axis=1), jnp.concatenate([bh, bh, bl], axis=0))
-
-
 def tile(j):
     return pl.ds(pl.multiple_of(j * LANES, LANES), LANES)
 
@@ -67,17 +63,26 @@
     lane = lane_iota()
     z_first = (lane % NZ) == 0
     upper = lane >= NZ
-    previous = src[slot, :, (tiles - 1) * LANES :]
     octets = src.shape[1] // 8
-    for j in range(tiles):
-        at = slice(j * LANES, (j + 1) * LANES)
-        here = src[slot, :, at]
-        upwind = src[slot - 1, :, at]
-        below_y = pltpu.roll(jnp.where(upper, previous, here), NZ, 1)
-        below_z = jnp.where(z_first, pltpu.roll(here, NZ + 1, 1), pltpu.roll(here, 1, 1))
-        cx, cy, cz = (jnp.concatenate([rates[c, plane, :, at]] * octets, axis=0) for c in range(3))
-        dst[slot, :, at] = here - cx * (here - upwind) - cy * (here - below_y) - cz * (here - below_z)
-        previous = here
+
+    def at(j):
+        j = (j + tiles) % tiles
+        return slice(j * LANES, (j + 1) * LANES)
+
+    for base in range(0, tiles, BATCH):
+        these = range(base, min(base + BATCH, tiles))
+        here = [src[slot, :, at(j)] for j in (base - 1, *these)]
+        upwind = [src[slot - 1, :, at(j)] for j in these]
+        below_y = [pltpu.roll(jnp.where(upper, x, y), NZ, 1) for x, y in zip(here, here[1:])]
+        here = here[1:]
+        one = [pltpu.roll(x, 1, 1) for x in here]
+        wrapped = [pltpu.roll(x, NZ + 1, 1) for x in here]
+        below_z = [jnp.where(z_first, x, y) for x, y in zip(wrapped, one)]
+        for j, u, ux, uy, uz in zip(these, here, upwind, below_y, below_z):
+            cx, cy, cz = (
+                jnp.concatenate([rates[c, plane, :, at(j)]] * octets, axis=0) for c in range(3)
+            )
+            dst[slot, :, at(j)] = u - cx * (u - ux) - cy * (u - uy) - cz * (u - uz)
 
 
 def fill(rates, wide):
@@ -205,7 +210,7 @@
         squared = jnp.where(slot < count[i], 1.0 / (errors[i] * (MEMBERS - 1.0)), 0.0)
         entry = jnp.where(is_value, squared * values[i], squared)
         entry = jnp.where(xs // PLANES == slab, entry, 0.0)
-        one, rest = split(entry)
+        one, _ = split(entry)
         two, three = split(entry - one.astype(F32))
         sums = dot(jnp.concatenate([one, two, three], axis=0), hits, True)
         total = sums[:rows] + sums[rows : 2 * rows] + sums[2 * rows :]
@@ -223,9 +228,13 @@
     return top, low
 
 
-def unpack(top, low):
+def every(function, *lists):
+    return [function(*x) for x in zip(*lists)]
+
+
+def lower_blocks(top, low):
     lane = lane_iota()
-    lower = jnp.concatenate(
+    return jnp.concatenate(
         [
             jnp.where(lane < 32, pltpu.roll(top, 32, 1), 0.0),
             jnp.where(lane < 64, low, 0.0),
@@ -235,14 +244,18 @@
         ],
         axis=0,
     )
-    upper = lower.T
+
+
+def unpack(tops, lows):
     row = lax.broadcasted_iota(jnp.int32, (LANES, LANES), 0)
     col = lax.broadcasted_iota(jnp.int32, (LANES, LANES), 1)
-    return jnp.where(row // 32 >= col // 32, lower, upper)
+    lower = every(lower_blocks, tops, lows)
+    upper = [x.T for x in lower]
+    return [jnp.where(row // 32 >= col // 32, x, y) for x, y in zip(lower, upper)]
 
 
 def gram_kernel(half, fields, maps, out, anomaly, high, low, mean):
-    groups, members = fields.shape[0] // half, fields.shape[1]
+    groups = fields.shape[0] // half
     blocks = maps.shape[0]
     for s in range(half):
         for t in range(fields.shape[2] // LANES):
@@ -294,47 +307,61 @@
 
     def each(body):
         def several(j, carry):
-            for e in range(batch):
-                body(j * batch + e)
+            at = [j * batch + e for e in range(batch)]
+            for i, (a, z) in zip(at, body(at)):
+                if a is not None:
+                    left[i] = a
+                if z is not None:
+                    right[i] = z
             return carry
 
         lax.fori_loop(0, steps, several, 0)
 
-    def start(i):
-        base = pl.multiple_of(i * PACKED, 8)
-        top = mine[pl.ds(base, 32), :] + other[pl.ds(base, 32), :]
-        low = mine[pl.ds(base + 32, 16), :] + other[pl.ds(base + 32, 16), :]
-        g = identity + unpack(top, low)
-        fro = jnp.sqrt(jnp.sum(jnp.sum(g * g, axis=0, keepdims=True), axis=1, keepdims=True))
-        scale[i] = jnp.broadcast_to(fro, (8, LANES))
-        left[i] = g * (1.0 / fro)
-
-    def second(i):
-        a = left[i]
-        middle = 1.5 * identity - 0.5 * a
-        left[i] = dot3(split(a), split(middle))
-        right[i] = middle
-
-    def iterate(i):
-        aa, zz = split(left[i]), split(right[i])
-        middle = split(1.5 * identity - 0.5 * dot3(zz, aa))
-        left[i] = dot3(aa, middle)
-        right[i] = dot3(middle, zz)
-
-    def last(i):
-        zz = split(right[i])
-        middle = split(1.5 * identity - 0.5 * dot3(zz, split(left[i])))
-        right[i] = dot3(middle, zz)
-
-    def finish(i):
-        transform = right[i, :MEMBERS] * (1.0 / jnp.sqrt(scale[i, :1]))
-        at = pl.ds(blocks * PACKED + i, 1)
-        inner = jnp.sum(transform * (mine[at, :] + other[at, :]), axis=1, keepdims=True)
-        top, low = pack(transform)
-        base = pl.multiple_of(i * PACKED, 8)
-        out[pl.ds(base, 32), :] = top
-        out[pl.ds(base + 32, 16), :] = low
-        out[at, :] = jnp.sum(transform * inner, axis=0, keepdims=True)
+    def middle(p):
+        return split(1.5 * identity - 0.5 * p)
+
+    def start(at):
+        bases = [pl.multiple_of(i * PACKED, 8) for i in at]
+        tops = [mine[pl.ds(x, 32), :] + other[pl.ds(x, 32), :] for x in bases]
+        lows = [mine[pl.ds(x + 32, 16), :] + other[pl.ds(x + 32, 16), :] for x in bases]
+        grams = [identity + x for x in unpack(tops, lows)]
+        sums = [jnp.sum(g * g, axis=0, keepdims=True) for g in grams]
+        sums = [jnp.sum(x, axis=1, keepdims=True) for x in sums]
+        roots = [lax.rsqrt(x) for x in sums]
+        for i, x in zip(at, roots):
+            scale[i] = jnp.broadcast_to(x, (8, LANES))
+        return [(g * x, None) for g, x in zip(grams, roots)]
+
+    def second(at):
+        a = [left[i] for i in at]
+        m = [1.5 * identity - 0.5 * x for x in a]
+        return zip(every(dot3, every(split, a), every(split, m)), m)
+
+    def iterate(at):
+        a = [split(left[i]) for i in at]
+        z = [split(right[i]) for i in at]
+        m = every(middle, every(dot3, z, a))
+        return zip(every(dot3, a, m), every(dot3, m, z))
+
+    def last(at):
+        a = [split(left[i]) for i in at]
+        z = [split(right[i]) for i in at]
+        m = every(middle, every(dot3, z, a))
+        return [(None, x) for x in every(dot3, m, z)]
+
+    def finish(at):
+        rows = [pl.ds(blocks * PACKED + i, 1) for i in at]
+        done = [right[i, :MEMBERS] * jnp.sqrt(scale[i, :1]) for i in at]
+        vectors = [mine[x, :] + other[x, :] for x in rows]
+        inner = [jnp.sum(t * x, axis=1, keepdims=True) for t, x in zip(done, vectors)]
+        means = [jnp.sum(t * x, axis=0, keepdims=True) for t, x in zip(done, inner)]
+        packs = every(pack, done)
+        for i, x, m, (top, low) in zip(at, rows, means, packs):
+            base = pl.multiple_of(i * PACKED, 8)
+            out[pl.ds(base, 32), :] = top
+            out[pl.ds(base + 32, 16), :] = low
+            out[x, :] = m
+        return []
 
     def loop(k, carry):
         each(iterate)
@@ -353,11 +380,11 @@
     first = (lane % SPAN) < TILE_WIDTH
 
     def pair(i, carry):
-        sides = []
-        for e in range(2):
-            base = pl.multiple_of((2 * i + e) * PACKED, 8)
-            t = unpack(weights[pl.ds(base, 32), :], weights[pl.ds(base + 32, 16), :])[:MEMBERS]
-            sides.append(t + weights[pl.ds(blocks * PACKED + 2 * i + e, 1), :])
+        bases = [pl.multiple_of((2 * i + e) * PACKED, 8) for e in range(2)]
+        tops = [weights[pl.ds(x, 32), :] for x in bases]
+        sides = unpack(tops, [weights[pl.ds(x + 32, 16), :] for x in bases])
+        rows_at = [pl.ds(blocks * PACKED + 2 * i + e, 1) for e in range(2)]
+        sides = [t[:MEMBERS] + weights[x, :] for t, x in zip(sides, rows_at)]
         left = split(jnp.concatenate(sides, axis=1))
         filler = jnp.zeros((LANES - MEMBERS, LANES), F32)
         for s in range(half):
@@ -401,7 +428,7 @@
             out[:, :, tile(which * half + s)] = source[s]
 
 
-def call(kernel, outs, scratch, *args, specs=None, cost=None):
+def call(kernel, outs, scratch, *args, specs=None, cost=None, room=20):
     shapes = [jax.ShapeDtypeStruct(s, F32) for s in outs]
     return pl.pallas_call(
         kernel,
@@ -409,7 +436,7 @@
         in_specs=specs or [VMEM] * len(args),
         out_specs=[VMEM] * len(shapes) if len(shapes) > 1 else VMEM,
         scratch_shapes=scratch,
-        compiler_params=pltpu.CompilerParams(vmem_limit_bytes=56 * 1024 * 1024),
+        compiler_params=pltpu.CompilerParams(vmem_limit_bytes=room * 1024 * 1024),
         cost_estimate=cost,
     )(*args)
 
@@ -457,6 +484,7 @@
         initial_samples,
         transport_ratios,
         cost=work(10**7, 10**7),
+        room=22,
     )
     halo = shifted(edge, "slab", 1)
     map_shape = (blocks, 2 * half, 2 * LANES)
@@ -482,6 +510,7 @@
         zh,
         specs=[VMEM] * 3 + [SMEM],
         cost=work(10**7, 10**7),
+        room=22,
     )
     packed = (blocks * PACKED + blocks, LANES)
 
@@ -516,11 +545,12 @@
         )
 
     fields_send = spread(send)
-    gram_other = partner(gram(fields_send, map_recv))
+    gram_send = gram(fields_send, map_recv)
+    gram_other = partner(gram_send)
     fields_keep = spread(keep)
     gram_mine = gram(fields_keep, map_keep)
     weights = call(
-        functools.partial(solve_kernel, 8, blocks),
+        functools.partial(solve_kernel, blocks, blocks),
         [packed],
         [pltpu.VMEM((blocks, LANES, LANES), F32)] * 2 + [pltpu.VMEM((blocks, 8, LANES), F32)],
         gram_mine,
@@ -528,7 +558,8 @@
         cost=work(10**9, 10**6),
     )
     weights_other = partner(weights)
-    result_mine = spread(apply(fields_keep, weights))
+    applied = apply(fields_keep, weights)
+    result_mine = spread(applied)
     result_other = spread(apply(fields_send, weights_other))
     part = pl.BlockSpec((half, members, planes, LANES), lambda g: (g, 0, 0, 0))
     return pl.pallas_call(
@@ -583,7 +614,7 @@
     slab_count = lax.axis_size("slab")
     own_columns = total_columns // (group_count * slab_count)
     state = initial_samples
-    for section in range(STEPS):
+    for _ in range(STEPS):
         edge_plane = shifted(state[:, planes - 1 :], "slab", 1)
         upwind = jnp.concatenate([edge_plane, state[:, : planes - 1]], axis=1)
         state = advance(state, upwind, transport_ratios)
@@ -636,7 +667,7 @@
     fro_norm = jnp.sqrt(jnp.sum(gram * gram, axis=(1, 2)))
     iterate_a = gram / fro_norm[:, None, None]
     iterate_z = jnp.broadcast_to(identity, gram.shape)
-    for iteration in range(ITERS):
+    for _ in range(ITERS):
         middle = 1.5 * identity[None] - 0.5 * jnp.einsum(
             "bij,bjk->bik", iterate_z, iterate_a, precision=hi
         )

time: 305 us -> 276 us (0.905)
  Pallas kernels: 119 us -> 85.9 us
    pallas_call x8, Pallas kernels: 114 us -> 81.7 us  [call(): pl.pallas_call(kernel, out_shape=shapes if len(shapes) > 1 else shapes[0]...]
    unnamed x22 -> x20, local copies, waits for them, and re-layouts: 4.83 us -> 6.4 us
  transfers between devices with their start and end apart: 6 -> 6, of which waited for: 4 -> 4; matrix products, arithmetic and copies ran while one was open for 1% -> 1% of each run, Pallas kernels for 11% -> 9%
where the time goes in v1:
time: 276 us; the launch traced here: 275 us
  waiting for transfers between devices  105 us (38%)
  Pallas kernels  85.9 us (31%)
  blocking collectives  55.9 us (20%)
  starting transfers between devices  18.9 us (7%)
  local copies, waits for them, and re-layouts  9.53 us (3%)
    ppermute x4, waiting for transfers between devices, shifted(): return lax.ppermute(block, axis, route)  105 us
    pallas_call x8, Pallas kernels, call(): pl.pallas_call(kernel, out_shape=shapes if len(shapes) > 1 else shapes[0]...  81.7 us
    all_to_all x2, blocking collectives, spread(): lax.all_to_all(x, AXES, split_axis=0, concat_axis=0, tiled=True, axis_ind...  55.9 us
    ppermute x4, starting transfers between devices, shifted(): return lax.ppermute(block, axis, route)  10.7 us
    all_to_all x2, starting transfers between devices, spread(): lax.all_to_all(x, AXES, split_axis=0, concat_axis=0, tiled=True, axis_ind...  8.26 us
    unnamed x20, local copies, waits for them, and re-layouts  6.4 us
  transfers between devices with their start and end apart: 6, of which 4 were waited for; matrix products, arithmetic and copies ran while one was open for 1% of the time, Pallas kernels for 9%

profile of v1, /device:TPU:0, one launch (start us, length us, event | category | flops | bytes accessed | tf_op | source)
XLA Modules:
  0.0 275.0 jit_solution(11646629813746749182)
XLA Ops:
  0.0 1.9 copy-done.1
  1.9 1.0 copy-done.3
  2.9 13.0 %shard_map.82 = (f32[8,24,4096]{2,1,0:T(8,128)S(1)}, f32[6,24,4096]{2,1,0:T(8,128)}) custom-call(f32[24,8,4096]{2,1,0:T(8,128)S(1)} %copy-done.1, f32[3,8,4096]{2,1,0:T(8,128)S(1)} %copy-done.3), custom_call_target="tpu_custom_call" | custom-call | flops 10000000 | bytes 10000000 | tf_op jit(solution)/shard_map/pallas_call | solution.py:433
  15.9 3.0 %collective-permute-start = (f32[6,24,4096]{2,1,0:T(8,128)}, f32[6,24,4096]{2,1,0:T(8,128)}, u32[]{:S(2)}, u32[]{:S(2)}) collective-permute-start(f32[6,24,4096]{2,1,0:T(8,128)} %get-tuple-element.12), channel_id=1, source_target_pairs={{7,0},{0,1},{1,2},{2,3},{3,4},{4,5},{5,6},{6,7},{15,8},{8,9},{9,10... | collective-permute-start | bytes 7077896 | tf_op jit(solution)/shard_map/ppermute | solution.py:34
  18.9 54.6 %collective-permute-done.halo = f32[6,24,4096]{2,1,0:T(8,128)} collective-permute-done((f32[6,24,4096]{2,1,0:T(8,128)}, f32[6,24,4096]{2,1,0:T(8,128)}, u32[]{:S(2)}, u32[]{:S(2)}) %collective-permute-start) | collective-permute-done | bytes 2359328 | tf_op jit(solution)/shard_map/ppermute | solution.py:34
  73.5 20.9 %shard_map.83 = (f32[16,24,1152]{2,1,0:T(8,128)S(1)}, f32[16,24,1152]{2,1,0:T(8,128)S(1)}) custom-call(f32[8,24,4096]{2,1,0:T(8,128)S(1)} %get-tuple-element.11.skew, f32[6,24,4096]{2,1,0:T(8,128)} %collective-permute-done.halo, f32[3,8,4096]{2,1,0:T(8,128)S(1)} %copy-done.4, s32[1]{0:T(128)} %bitcast.zh), custom_call_target="tpu_custom_call" | custom-call | flops 10000000 | bytes 10000000 | tf_op jit(solution)/shard_map/pallas_call | solution.py:433
  94.4 26.1 %all_to_all.20.fields = f32[16,24,1152]{2,1,0:T(8,128)S(1)} all-to-all(f32[16,24,1152]{2,1,0:T(8,128)S(1)} %get-tuple-element.15), channel_id=1, replica_groups={{0,1,2,3,8,9,10,11,16,17,18,19,24,25,26,27},{4,5,6,7,12,13,14,15,20,21,..., dimensions={0} | all-to-all | bytes 3538944 | tf_op jit(solution)/shard_map/all_to_all | solution.py:471
  120.5 3.8 %all-to-all-start = ((f32[16,24,1152]{2,1,0:T(8,128)}), f32[16,24,1152]{2,1,0:T(8,128)S(1)}, u32[]{:S(2)}, u32[]{:S(2)}) async-start(f32[16,24,1152]{2,1,0:T(8,128)} %copy-done.2), calls=%async_computation | async-start | bytes 3538944 | tf_op jit(solution)/shard_map/all_to_all | solution.py:471
  127.6 4.0 %shard_map.84 = (f32[16,8,256]{2,1,0:T(8,128)S(1)}, f32[16,8,256]{2,1,0:T(8,128)S(1)}) custom-call(f32[16,1,512]{2,1,0:T(1,128)S(1)} %broadcast_in_dim.12.values, f32[16,1,512]{2,1,0:T(1,128)S(1)} %broadcast_in_dim.13.errors, s32[16,1,512]{2,1,0:T(1,128)S(1)} %broadcast_in_dim.14.x, s32[16,1,512]{2,1,0:T(1,128)S(1)} %broadcast_in_dim.15.column, ...), custom_call_target="tpu_custom_call" | custom-call | flops 100000000 | bytes 1000000 | tf_op jit(solution)/shard_map/pallas_call | solution.py:433
  132.3 1.7 collective-permute-start.1
  134.0 13.6 %collective-permute-done.1.maps = f32[16,8,256]{2,1,0:T(8,128)S(1)} collective-permute-done((f32[16,8,256]{2,1,0:T(8,128)S(1)}, f32[16,8,256]{2,1,0:T(8,128)S(1)}, u32[]{:S(2)}, u32[]{:S(2)}) %collective-permute-start.1) | collective-permute-done | bytes 131104 | tf_op jit(solution)/shard_map/ppermute | solution.py:34
  147.6 5.8 %shard_map.86 = f32[784,128]{1,0:T(8,128)} custom-call(f32[16,24,1152]{2,1,0:T(8,128)S(1)} %all_to_all.20.fields, f32[16,8,256]{2,1,0:T(8,128)S(1)} %collective-permute-done.1.maps), custom_call_target="tpu_custom_call" | custom-call | flops 1000000000 | bytes 4000000 | tf_op jit(solution)/shard_map/pallas_call | solution.py:433
  153.4 3.4 %collective-permute-start.2 = (f32[784,128]{1,0:T(8,128)}, f32[784,128]{1,0:T(8,128)}, u32[]{:S(2)}, u32[]{:S(2)}) collective-permute-start(f32[784,128]{1,0:T(8,128)} %shard_map.86), channel_id=1, source_target_pairs={{4,0},{5,1},{6,2},{7,3},{0,4},{1,5},{2,6},{3,7},{12,8},{13,9},{14,... | collective-permute-start | bytes 1204232 | tf_op jit(solution)/shard_map/ppermute | solution.py:34
  157.7 5.0 %shard_map.85.mine = f32[784,128]{1,0:T(8,128)S(1)} custom-call(f32[16,24,1152]{2,1,0:T(8,128)S(1)} %all-to-all-done.fields, f32[16,8,256]{2,1,0:T(8,128)S(1)} %copy-done.9), custom_call_target="tpu_custom_call" | custom-call | flops 1000000000 | bytes 4000000 | tf_op jit(solution)/shard_map/pallas_call | solution.py:433
  162.8 12.2 %collective-permute-done.2.other = f32[784,128]{1,0:T(8,128)} collective-permute-done((f32[784,128]{1,0:T(8,128)}, f32[784,128]{1,0:T(8,128)}, u32[]{:S(2)}, u32[]{:S(2)}) %collective-permute-start.2) | collective-permute-done | bytes 401440 | tf_op jit(solution)/shard_map/ppermute | solution.py:34
  175.0 12.3 %shard_map.87.weights = f32[784,128]{1,0:T(8,128)S(1)} custom-call(f32[784,128]{1,0:T(8,128)S(1)} %shard_map.85.mine, f32[784,128]{1,0:T(8,128)} %collective-permute-done.2.other), custom_call_target="tpu_custom_call" | custom-call | flops 1000000000 | bytes 1000000 | tf_op jit(solution)/shard_map/pallas_call | solution.py:433
  187.3 10.3 %shard_map.88 = f32[16,24,8,128]{3,2,1,0:T(8,128)S(1)} custom-call(f32[16,24,1152]{2,1,0:T(8,128)S(1)} %all-to-all-done.fields, f32[784,128]{1,0:T(8,128)S(1)} %shard_map.87.weights, s32[96]{0:T(128)S(1)} %copy-done.6), custom_call_target="tpu_custom_call" | custom-call | flops 1000000000 | bytes 4000000 | tf_op jit(solution)/shard_map/pallas_call | solution.py:433
  197.7 1.1 copy-done
  199.6 4.4 %all-to-all-start.2 = ((f32[16,24,8,128]{3,2,1,0:T(8,128)}), f32[16,24,8,128]{3,2,1,0:T(8,128)}, u32[]{:S(2)}, u32[]{:S(2)}) async-start(f32[16,24,8,128]{3,2,1,0:T(8,128)} %copy-done), calls=%async_computation.2 | async-start | bytes 3145728 | tf_op jit(solution)/shard_map/all_to_all | solution.py:471
  204.0 2.5 collective-permute-start.3
  206.5 24.2 %collective-permute-done.3.weights = f32[784,128]{1,0:T(8,128)S(1)} collective-permute-done((f32[784,128]{1,0:T(8,128)}, f32[784,128]{1,0:T(8,128)S(1)}, u32[]{:S(2)}, u32[]{:S(2)}) %collective-permute-start.3) | collective-permute-done | bytes 401440 | tf_op jit(solution)/shard_map/ppermute | solution.py:34
  230.7 10.3 %shard_map.89 = f32[16,24,8,128]{3,2,1,0:T(8,128)S(1)} custom-call(f32[16,24,1152]{2,1,0:T(8,128)S(1)} %all_to_all.20.fields, f32[784,128]{1,0:T(8,128)S(1)} %collective-permute-done.3.weights, s32[96]{0:T(128)S(1)} %copy-done.6), custom_call_target="tpu_custom_call" | custom-call | flops 1000000000 | bytes 4000000 | tf_op jit(solution)/shard_map/pallas_call | solution.py:433
  241.0 29.7 %all_to_all.21.other = f32[16,24,8,128]{3,2,1,0:T(8,128)} all-to-all(f32[16,24,8,128]{3,2,1,0:T(8,128)S(1)} %shard_map.89), channel_id=1, replica_groups={{0,1,2,3,8,9,10,11,16,17,18,19,24,25,26,27},{4,5,6,7,12,13,14,15,20,21,..., dimensions={0} | all-to-all | bytes 3145728 | tf_op jit(solution)/shard_map/all_to_all | solution.py:471
  270.8 4.2 %shard_map.90 = f32[24,8,4096]{2,1,0:T(8,128)} custom-call(f32[16,24,8,128]{3,2,1,0:T(8,128)} %all-to-all-done.2.mine, f32[16,24,8,128]{3,2,1,0:T(8,128)} %all_to_all.21.other, s32[1]{0:T(128)} %bitcast.zh), custom_call_target="tpu_custom_call" | custom-call | tf_op jit(solution)/shard_map/pallas_call | solution.py:565
  (23 shorter events, 5.5 us)
Async XLA Ops:
  0.0 1.9 copy-start.1
  1.9 1.0 copy-start.3
  2.9 70.6 %copy-start.4 = (f32[3,8,4096]{2,1,0:T(8,128)S(1)}, f32[3,8,4096]{2,1,0:T(8,128)}, u32[]{:S(2)}) copy-start(f32[3,8,4096]{2,1,0:T(8,128)} %ratios.3) | copy-start | bytes 1179652
  15.9 57.6 %collective-permute-start = (f32[6,24,4096]{2,1,0:T(8,128)}, f32[6,24,4096]{2,1,0:T(8,128)}, u32[]{:S(2)}, u32[]{:S(2)}) collective-permute-start(f32[6,24,4096]{2,1,0:T(8,128)} %get-tuple-element.12), channel_id=1, source_target_pairs={{7,0},{0,1},{1,2},{2,3},{3,4},{4,5},{5,6},{6,7},{15,8},{8,9},{9,10... | collective-permute-start | bytes 7077896 | tf_op jit(solution)/shard_map/ppermute | solution.py:34
  94.4 26.1 %copy-start.2 = (f32[16,24,1152]{2,1,0:T(8,128)}, f32[16,24,1152]{2,1,0:T(8,128)S(1)}, u32[]{:S(2)}) copy-start(f32[16,24,1152]{2,1,0:T(8,128)S(1)} %get-tuple-element.13) | copy-start | bytes 5308420
  120.5 7.0 %copy-start.7 = (s32[16]{0:T(128)S(1)}, s32[16]{0:T(128)}, u32[]{:S(2)}) copy-start(s32[16]{0:T(128)} %count.1) | copy-start | bytes 196
  120.5 36.3 %all-to-all-start = ((f32[16,24,1152]{2,1,0:T(8,128)}), f32[16,24,1152]{2,1,0:T(8,128)S(1)}, u32[]{:S(2)}, u32[]{:S(2)}) async-start(f32[16,24,1152]{2,1,0:T(8,128)} %copy-done.2), calls=%async_computation | async-start | bytes 3538944 | tf_op jit(solution)/shard_map/all_to_all | solution.py:471
  131.6 0.7 copy-start.8
  132.3 15.4 %collective-permute-start.1 = (f32[16,8,256]{2,1,0:T(8,128)S(1)}, f32[16,8,256]{2,1,0:T(8,128)S(1)}, u32[]{:S(2)}, u32[]{:S(2)}) collective-permute-start(f32[16,8,256]{2,1,0:T(8,128)S(1)} %get-tuple-element.16), channel_id=1, source_target_pairs={{4,0},{5,1},{6,2},{7,3},{0,4},{1,5},{2,6},{3,7},{12,8},{13,9},{14,... | collective-permute-start | bytes 393224 | tf_op jit(solution)/shard_map/ppermute | solution.py:34
  153.4 21.6 %collective-permute-start.2 = (f32[784,128]{1,0:T(8,128)}, f32[784,128]{1,0:T(8,128)}, u32[]{:S(2)}, u32[]{:S(2)}) collective-permute-start(f32[784,128]{1,0:T(8,128)} %shard_map.86), channel_id=1, source_target_pairs={{4,0},{5,1},{6,2},{7,3},{0,4},{1,5},{2,6},{3,7},{12,8},{13,9},{14,... | collective-permute-start | bytes 1204232 | tf_op jit(solution)/shard_map/ppermute | solution.py:34
  156.8 0.9 copy-start.9
  162.8 24.6 %copy-start.6 = (s32[96]{0:T(128)S(1)}, s32[96]{0:T(128)}, u32[]{:S(2)}) copy-start(s32[96]{0:T(128)} %assignment.3) | copy-start | bytes 1156
  197.7 1.1 copy-start
  198.8 0.8 copy-start.5
  199.6 41.4 %all-to-all-start.2 = ((f32[16,24,8,128]{3,2,1,0:T(8,128)}), f32[16,24,8,128]{3,2,1,0:T(8,128)}, u32[]{:S(2)}, u32[]{:S(2)}) async-start(f32[16,24,8,128]{3,2,1,0:T(8,128)} %copy-done), calls=%async_computation.2 | async-start | bytes 3145728 | tf_op jit(solution)/shard_map/all_to_all | solution.py:471
  204.0 26.7 %collective-permute-start.3 = (f32[784,128]{1,0:T(8,128)}, f32[784,128]{1,0:T(8,128)S(1)}, u32[]{:S(2)}, u32[]{:S(2)}) collective-permute-start(f32[784,128]{1,0:T(8,128)} %copy-done.5), channel_id=1, source_target_pairs={{4,0},{5,1},{6,2},{7,3},{0,4},{1,5},{2,6},{3,7},{12,8},{13,9},{14,... | collective-permute-start | bytes 1204232 | tf_op jit(solution)/shard_map/ppermute | solution.py:34

commit v2 on v1

--- a/solution.py
+++ b/solution.py
@@ -20,7 +20,7 @@
 PLANES = 8
 SPAN = 16
 PACKED = 48
-BATCH = 4
+BATCH = 8
 F32 = jnp.float32
 BF16 = jnp.bfloat16
 AXES = ("group", "slab")
@@ -141,7 +141,8 @@
     return v
 
 
-def second_kernel(half, slabs, skew, halo, ratios, zh, keep, send, a, b, rates):
+def second_kernel(half, slabs, octet, skew, halo, ratios, zh, *refs):
+    keep_out, send_out, keep, send, a, b, rates, sems = refs[-8:]
     tiles = a.shape[2] // LANES
     fill(ratios, rates)
     for p in range(STEPS):
@@ -168,29 +169,48 @@
 
     lane = lane_iota()
     block = lane // SPAN
+    members = skew.shape[1]
 
     def load(p, j):
-        return a[p + 1, :, tile(j)] if p < STEPS else skew[p, :, tile(j)]
-
-    def moved(p, j):
-        before = lax.rem(j + (tiles - 1), tiles)
-        return pltpu.roll(jnp.where(lane >= LANES - HC, load(p, before), load(p, j)), HC, 1)
+        at = tile(lax.rem(j + tiles, tiles))
+        return a[p + 1, :, at] if p < STEPS else skew[p, :, at]
+
+    def moved(p, base):
+        parts = [load(p, base + t) for t in range(-1, half + 1)]
+        here, before = jnp.concatenate(parts[1:], axis=0), jnp.concatenate(parts[:-1], axis=0)
+        return pltpu.roll(jnp.where(lane >= LANES - HC, before, here), HC, 1)
 
     for out, which in ((send, 1 - zh[0]), (keep, zh[0])):
 
-        def chunk(q, carry, out=out, which=which):
-            j = lax.div(q, half) * slabs + which * half + lax.rem(q, half)
-            groups = exchange_blocks([moved(p, j) for p in range(PLANES)])
-            for t in range(8):
-                out[q, :, t * LANES : (t + 1) * LANES] = groups[t]
-            after = lax.rem(j + 1, tiles)
-            last = moved(0, after)
+        def chunk(g, carry, out=out, which=which):
+            rows = [moved(p, g * slabs + which * half) for p in range(PLANES)]
+            count = half * members
+            after = [x[count:] for x in rows]
+            last = after[0]
             for p in range(1, PLANES):
-                last = jnp.where(block == p, pltpu.roll(moved(p, after), SPAN * p, 1), last)
-            out[q, :, 8 * LANES :] = last
+                last = jnp.where(block == p, pltpu.roll(after[p], SPAN * p, 1), last)
+            groups = exchange_blocks([x[:count] for x in rows])
+            for i in range(half):
+                for t in range(8):
+                    out[g * half + i, :, t * LANES : (t + 1) * LANES] = groups[t][
+                        i * members : (i + 1) * members
+                    ]
+            for i in range(half - 1):
+                out[g * half + i, :, 8 * LANES :] = groups[0][(i + 1) * members : (i + 2) * members]
+            out[g * half + half - 1, :, 8 * LANES :] = last
             return carry
 
-        lax.fori_loop(0, out.shape[0], chunk, 0)
+        lax.fori_loop(0, out.shape[0] // half, chunk, 0)
+
+    at = pl.ds(octet * members, members)
+    copies = [
+        pltpu.make_async_copy(send, send_out.at[:, at, :], sems.at[0]),
+        pltpu.make_async_copy(keep, keep_out.at[:, at, :], sems.at[1]),
+    ]
+    for copy in copies:
+        copy.start()
+    for copy in copies:
+        copy.wait()
 
 
 def map_kernel(half, values, errors, x, column, count, zh, keep, send):
@@ -254,13 +274,18 @@
     return [jnp.where(row // 32 >= col // 32, x, y) for x, y in zip(lower, upper)]
 
 
-def gram_kernel(half, fields, maps, out, anomaly, high, low, mean):
-    groups = fields.shape[0] // half
+def member_rows(fields, half, s, at):
+    groups = fields[0].shape[0] // half
+    return jnp.concatenate([f[g * half + s, :, at] for g in range(groups) for f in fields], axis=0)
+
+
+def gram_kernel(half, octets, *refs):
+    fields, (maps, out, anomaly, high, low, mean) = refs[:octets], refs[octets:]
     blocks = maps.shape[0]
     for s in range(half):
-        for t in range(fields.shape[2] // LANES):
+        for t in range(fields[0].shape[2] // LANES):
             at = slice(t * LANES, (t + 1) * LANES)
-            f = jnp.concatenate([fields[g * half + s, :, at] for g in range(groups)], axis=0)
+            f = member_rows(fields, half, s, at)
             average = jnp.sum(f, axis=0, keepdims=True) / MEMBERS
             f = f - average
             mean[s, :, at] = average
@@ -374,8 +399,9 @@
     each(finish)
 
 
-def apply_kernel(half, blocks, fields, weights, assignment, out, result, planar):
-    groups, members = fields.shape[0] // half, fields.shape[1]
+def apply_kernel(half, blocks, octets, *refs):
+    fields, (weights, assignment, out, result, planar) = refs[:octets], refs[octets:]
+    members = out.shape[1]
     lane = lane_iota()
     first = (lane % SPAN) < TILE_WIDTH
 
@@ -389,9 +415,7 @@
         filler = jnp.zeros((LANES - MEMBERS, LANES), F32)
         for s in range(half):
 
-            def rows(at):
-                return jnp.concatenate([fields[g * half + s, :, at] for g in range(groups)], axis=0)
-
+            rows = functools.partial(member_rows, fields, half, s)
             x = jnp.where(
                 first,
                 pltpu.roll(rows(tile(i)), LANES - TILE_WIDTH, 1),
@@ -428,11 +452,12 @@
             out[:, :, tile(which * half + s)] = source[s]
 
 
-def call(kernel, outs, scratch, *args, specs=None, cost=None, room=20):
+def call(kernel, outs, scratch, *args, specs=None, cost=None, room=20, grid=()):
     shapes = [jax.ShapeDtypeStruct(s, F32) for s in outs]
     return pl.pallas_call(
         kernel,
         out_shape=shapes if len(shapes) > 1 else shapes[0],
+        grid=grid,
         in_specs=specs or [VMEM] * len(args),
         out_specs=[VMEM] * len(shapes) if len(shapes) > 1 else VMEM,
         scratch_shapes=scratch,
@@ -475,19 +500,24 @@
     def partner(x):
         return shifted(x, "slab", half)
 
-    whole = (planes, members, columns)
+    octets = members // 8
+    map_shape = (blocks, 2 * half, 2 * LANES)
+    whole = (planes, 8, columns)
     wide = [pltpu.VMEM((3, planes, 8, columns), F32)]
-    skew, edge = call(
-        first_kernel,
-        [whole, (STEPS, members, columns)],
-        [pltpu.VMEM(whole, F32)] * 2 + wide,
-        initial_samples,
-        transport_ratios,
-        cost=work(10**7, 10**7),
-        room=22,
-    )
-    halo = shifted(edge, "slab", 1)
-    map_shape = (blocks, 2 * half, 2 * LANES)
+    firsts, halos = [], []
+    for c in range(octets):
+        skew, edge = call(
+            first_kernel,
+            [whole, (STEPS, 8, columns)],
+            [pltpu.VMEM(whole, F32)] * 2 + wide,
+            initial_samples,
+            transport_ratios,
+            specs=[pl.BlockSpec((8, planes, columns), lambda i, c=c: (c, 0, 0)), VMEM],
+            cost=work(10**7, 4 * 10**6),
+            grid=(1,),
+        )
+        firsts.append(skew)
+        halos.append(shifted(edge, "slab", 1))
     map_keep, map_send = call(
         functools.partial(map_kernel, half),
         [map_shape, map_shape],
@@ -499,24 +529,31 @@
         cost=work(10**8, 10**6),
     )
     map_recv = partner(map_send)
-    payload = (peers, members, width)
-    keep, send = call(
-        functools.partial(second_kernel, half, slabs),
-        [payload, payload],
-        [pltpu.VMEM((STEPS + 1, members, columns), F32)] * 2 + wide,
-        skew,
-        halo,
-        transport_ratios,
-        zh,
-        specs=[VMEM] * 3 + [SMEM],
-        cost=work(10**7, 10**7),
-        room=22,
-    )
+    payload = jax.ShapeDtypeStruct((peers, members, width), F32)
+    part = pltpu.VMEM((peers, 8, width), F32)
+    anywhere = pl.BlockSpec(memory_space=pl.ANY)
+    held = []
+    for c in range(octets):
+        held = pl.pallas_call(
+            functools.partial(second_kernel, half, slabs, c),
+            out_shape=[payload, payload],
+            in_specs=[VMEM] * 3 + [SMEM] + [anywhere] * len(held),
+            out_specs=[anywhere] * 2,
+            scratch_shapes=[part, part]
+            + [pltpu.VMEM((STEPS + 1, 8, columns), F32)] * 2
+            + wide
+            + [pltpu.SemaphoreType.DMA((2,))],
+            input_output_aliases={4: 0, 5: 1} if held else {},
+            compiler_params=pltpu.CompilerParams(vmem_limit_bytes=20 * 1024 * 1024),
+            cost_estimate=work(10**7, 4 * 10**6),
+        )(firsts[c], halos[c], transport_ratios, zh, *held)
+    fields_send = [spread(held[1])]
+    fields_keep = [spread(held[0])]
     packed = (blocks * PACKED + blocks, LANES)
 
     def gram(fields, maps):
         return call(
-            functools.partial(gram_kernel, half),
+            functools.partial(gram_kernel, half, 1),
             [packed],
             [
                 pltpu.VMEM((half, MEMBERS, width), F32),
@@ -524,30 +561,28 @@
                 pltpu.VMEM((half, LANES, width), BF16),
                 pltpu.VMEM((half, 1, width), F32),
             ],
-            fields,
+            *fields,
             maps,
             cost=work(10**9, 4 * 10**6),
         )
 
     def apply(fields, weights):
         return call(
-            functools.partial(apply_kernel, half, blocks),
+            functools.partial(apply_kernel, half, blocks, 1),
             [(peers, members, planes, LANES)],
             [
                 pltpu.VMEM((half, blocks // 2, MEMBERS, LANES), F32),
                 pltpu.VMEM((PLANES * MEMBERS, LANES), F32),
             ],
-            fields,
+            *fields,
             weights,
             assignment,
             specs=[VMEM] * 2 + [SMEM],
             cost=work(10**9, 4 * 10**6),
         )
 
-    fields_send = spread(send)
     gram_send = gram(fields_send, map_recv)
     gram_other = partner(gram_send)
-    fields_keep = spread(keep)
     gram_mine = gram(fields_keep, map_keep)
     weights = call(
         functools.partial(solve_kernel, blocks, blocks),

time: 276 us -> 258 us (0.935)
  waiting for transfers between devices: 105 us -> 67.5 us
  Pallas kernels: 85.9 us -> 98.4 us
  starting transfers between devices: 18.9 us -> 22.7 us
    ppermute x4 -> x6, waiting for transfers between devices: 105 us -> 67.5 us  [shifted(): return lax.ppermute(block, axis, route)]
    pallas_call x0 -> x3, Pallas kernels: none -> 27.4 us  [planned(): pl.pallas_call(functools.partial(second_kernel, half, slabs, c), out_shap...]
    pallas_call x8 -> x9, Pallas kernels: 81.7 us -> 66.8 us  [call(): pl.pallas_call(kernel, out_shape=shapes if len(shapes) > 1 else shapes[0]...]
    ppermute x4 -> x6, starting transfers between devices: 10.7 us -> 14.1 us  [shifted(): return lax.ppermute(block, axis, route)]
    unnamed x20 -> x28, local copies, waits for them, and re-layouts: 6.4 us -> 8.37 us
  transfers between devices with their start and end apart: 6 -> 8, of which waited for: 4 -> 6; matrix products, arithmetic and copies ran while one was open for 1% -> 1% of each run, Pallas kernels for 9% -> 22%
where the time goes in v2:
time: 258 us; the launch traced here: 257 us
  Pallas kernels  98.4 us (38%)
  waiting for transfers between devices  67.5 us (26%)
  blocking collectives  56.4 us (22%)
  starting transfers between devices  22.7 us (9%)
  local copies, waits for them, and re-layouts  11.5 us (4%)
    ppermute x6, waiting for transfers between devices, shifted(): return lax.ppermute(block, axis, route)  67.5 us
    pallas_call x9, Pallas kernels, call(): pl.pallas_call(kernel, out_shape=shapes if len(shapes) > 1 else shapes[0]...  66.8 us
    all_to_all x2, blocking collectives, spread(): lax.all_to_all(x, AXES, split_axis=0, concat_axis=0, tiled=True, axis_ind...  56.4 us
    pallas_call x3, Pallas kernels, planned(): pl.pallas_call(functools.partial(second_kernel, half, slabs, c), out_shap...  27.4 us
    ppermute x6, starting transfers between devices, shifted(): return lax.ppermute(block, axis, route)  14.1 us
    all_to_all x2, starting transfers between devices, spread(): lax.all_to_all(x, AXES, split_axis=0, concat_axis=0, tiled=True, axis_ind...  8.57 us
    unnamed x28, local copies, waits for them, and re-layouts  8.37 us
  transfers between devices with their start and end apart: 8, of which 6 were waited for; matrix products, arithmetic and copies ran while one was open for 1% of the time, Pallas kernels for 22%

profile of v2, /device:TPU:0, one launch (start us, length us, event | category | flops | bytes accessed | tf_op | source)
XLA Modules:
  0.0 256.7 jit_solution(11443761188628902562)
XLA Ops:
  2.9 6.3 %shard_map.84 = (f32[8,8,4096]{2,1,0:T(8,128)S(1)}, f32[6,8,4096]{2,1,0:T(8,128)}) custom-call(f32[24,8,4096]{2,1,0:T(8,128)S(1)} %copy-done, f32[3,8,4096]{2,1,0:T(8,128)S(1)} %copy-done.1), custom_call_target="tpu_custom_call" | custom-call | flops 10000000 | bytes 4000000 | tf_op jit(solution)/shard_map/pallas_call | solution.py:457
  12.2 6.3 %shard_map.83 = (f32[8,8,4096]{2,1,0:T(8,128)S(1)}, f32[6,8,4096]{2,1,0:T(8,128)}) custom-call(f32[24,8,4096]{2,1,0:T(8,128)S(1)} %copy-done, f32[3,8,4096]{2,1,0:T(8,128)S(1)} %copy-done.1), custom_call_target="tpu_custom_call" | custom-call | flops 10000000 | bytes 4000000 | tf_op jit(solution)/shard_map/pallas_call | solution.py:457
  21.1 6.4 %shard_map.82 = (f32[8,8,4096]{2,1,0:T(8,128)S(1)}, f32[6,8,4096]{2,1,0:T(8,128)}) custom-call(f32[24,8,4096]{2,1,0:T(8,128)S(1)} %copy-done, f32[3,8,4096]{2,1,0:T(8,128)S(1)} %copy-done.1), custom_call_target="tpu_custom_call" | custom-call | flops 10000000 | bytes 4000000 | tf_op jit(solution)/shard_map/pallas_call | solution.py:457
  29.9 4.0 %collective-permute-done.2.halo = f32[6,8,4096]{2,1,0:T(8,128)} collective-permute-done((f32[6,8,4096]{2,1,0:T(8,128)}, f32[6,8,4096]{2,1,0:T(8,128)}, u32[]{:S(2)}, u32[]{:S(2)}) %collective-permute-start.2) | collective-permute-done | bytes 786464 | tf_op jit(solution)/shard_map/ppermute | solution.py:34
  34.0 9.1 %shard_map.85 = (f32[16,24,1152]{2,1,0:T(8,128)}, f32[16,24,1152]{2,1,0:T(8,128)S(1)}) custom-call(f32[8,8,4096]{2,1,0:T(8,128)S(1)} %get-tuple-element.23.skew, f32[6,8,4096]{2,1,0:T(8,128)} %collective-permute-done.2.halo, f32[3,8,4096]{2,1,0:T(8,128)S(1)} %copy-done.2, s32[1]{0:T(128)} %bitcast.zh), custom_call_target="tpu_custom_call" | custom-call | flops 10000000 | bytes 4000000 | tf_op jit(solution)/shard_map/pallas_call | solution.py:537
  43.1 7.7 %collective-permute-done.1.halo = f32[6,8,4096]{2,1,0:T(8,128)} collective-permute-done((f32[6,8,4096]{2,1,0:T(8,128)}, f32[6,8,4096]{2,1,0:T(8,128)}, u32[]{:S(2)}, u32[]{:S(2)}) %collective-permute-start.1) | collective-permute-done | bytes 786464 | tf_op jit(solution)/shard_map/ppermute | solution.py:34
  50.8 9.2 %shard_map.86 = (f32[16,24,1152]{2,1,0:T(8,128)}, f32[16,24,1152]{2,1,0:T(8,128)S(1)}) custom-call(f32[8,8,4096]{2,1,0:T(8,128)S(1)} %copy-done.7, f32[6,8,4096]{2,1,0:T(8,128)} %collective-permute-done.1.halo, f32[3,8,4096]{2,1,0:T(8,128)S(1)} %copy-done.2, s32[1]{0:T(128)} %bitcast.zh, ...), custom_call_target="tpu_custom_call", output_to_operand_aliasing={{0}: (4, {}), {1}: (5, {})} | custom-call | flops 10000000 | bytes 4000000 | tf_op jit(solution)/shard_map/pallas_call | solution.py:537
  60.0 6.8 %collective-permute-done.halo = f32[6,8,4096]{2,1,0:T(8,128)} collective-permute-done((f32[6,8,4096]{2,1,0:T(8,128)}, f32[6,8,4096]{2,1,0:T(8,128)}, u32[]{:S(2)}, u32[]{:S(2)}) %collective-permute-start) | collective-permute-done | bytes 786464 | tf_op jit(solution)/shard_map/ppermute | solution.py:34
  66.8 9.1 %shard_map.87 = (f32[16,24,1152]{2,1,0:T(8,128)}, f32[16,24,1152]{2,1,0:T(8,128)S(1)}) custom-call(f32[8,8,4096]{2,1,0:T(8,128)S(1)} %copy-done.5, f32[6,8,4096]{2,1,0:T(8,128)} %collective-permute-done.halo, f32[3,8,4096]{2,1,0:T(8,128)S(1)} %copy-done.2, s32[1]{0:T(128)} %bitcast.zh, ...), custom_call_target="tpu_custom_call", output_to_operand_aliasing={{0}: (4, {}), {1}: (5, {})} | custom-call | flops 10000000 | bytes 4000000 | tf_op jit(solution)/shard_map/pallas_call | solution.py:537
  75.9 26.1 %all_to_all.20.refs_0_ = f32[16,24,1152]{2,1,0:T(8,128)S(1)} all-to-all(f32[16,24,1152]{2,1,0:T(8,128)S(1)} %get-tuple-element.31), channel_id=1, replica_groups={{0,1,2,3,8,9,10,11,16,17,18,19,24,25,26,27},{4,5,6,7,12,13,14,15,20,21,..., dimensions={0} | all-to-all | bytes 3538944 | tf_op jit(solution)/shard_map/all_to_all | solution.py:496
  102.1 4.0 %all-to-all-start = ((f32[16,24,1152]{2,1,0:T(8,128)}), f32[16,24,1152]{2,1,0:T(8,128)S(1)}, u32[]{:S(2)}, u32[]{:S(2)}) async-start(f32[16,24,1152]{2,1,0:T(8,128)} %get-tuple-element.29), calls=%async_computation | async-start | bytes 3538944 | tf_op jit(solution)/shard_map/all_to_all | solution.py:496
  109.3 4.0 %shard_map.88 = (f32[16,8,256]{2,1,0:T(8,128)S(1)}, f32[16,8,256]{2,1,0:T(8,128)S(1)}) custom-call(f32[16,1,512]{2,1,0:T(1,128)S(1)} %broadcast_in_dim.12.values, f32[16,1,512]{2,1,0:T(1,128)S(1)} %broadcast_in_dim.13.errors, s32[16,1,512]{2,1,0:T(1,128)S(1)} %broadcast_in_dim.14.x, s32[16,1,512]{2,1,0:T(1,128)S(1)} %broadcast_in_dim.15.column, ...), custom_call_target="tpu_custom_call" | custom-call | flops 100000000 | bytes 1000000 | tf_op jit(solution)/shard_map/pallas_call | solution.py:457
  115.7 13.2 %collective-permute-done.3.refs_1_ = f32[16,8,256]{2,1,0:T(8,128)S(1)} collective-permute-done((f32[16,8,256]{2,1,0:T(8,128)S(1)}, f32[16,8,256]{2,1,0:T(8,128)S(1)}, u32[]{:S(2)}, u32[]{:S(2)}) %collective-permute-start.3) | collective-permute-done | bytes 131104 | tf_op jit(solution)/shard_map/ppermute | solution.py:34
  128.9 5.8 %shard_map.90 = f32[784,128]{1,0:T(8,128)} custom-call(f32[16,24,1152]{2,1,0:T(8,128)S(1)} %all_to_all.20.refs_0_, f32[16,8,256]{2,1,0:T(8,128)S(1)} %collective-permute-done.3.refs_1_), custom_call_target="tpu_custom_call" | custom-call | flops 1000000000 | bytes 4000000 | tf_op jit(solution)/shard_map/pallas_call | solution.py:457
  134.7 3.4 %collective-permute-start.4 = (f32[784,128]{1,0:T(8,128)}, f32[784,128]{1,0:T(8,128)}, u32[]{:S(2)}, u32[]{:S(2)}) collective-permute-start(f32[784,128]{1,0:T(8,128)} %shard_map.90), channel_id=1, source_target_pairs={{4,0},{5,1},{6,2},{7,3},{0,4},{1,5},{2,6},{3,7},{12,8},{13,9},{14,... | collective-permute-start | bytes 1204232 | tf_op jit(solution)/shard_map/ppermute | solution.py:34
  139.0 5.0 %shard_map.89.mine = f32[784,128]{1,0:T(8,128)S(1)} custom-call(f32[16,24,1152]{2,1,0:T(8,128)S(1)} %all-to-all-done.refs_0_, f32[16,8,256]{2,1,0:T(8,128)S(1)} %copy-done.13), custom_call_target="tpu_custom_call" | custom-call | flops 1000000000 | bytes 4000000 | tf_op jit(solution)/shard_map/pallas_call | solution.py:457
  144.1 12.1 %collective-permute-done.4.other = f32[784,128]{1,0:T(8,128)} collective-permute-done((f32[784,128]{1,0:T(8,128)}, f32[784,128]{1,0:T(8,128)}, u32[]{:S(2)}, u32[]{:S(2)}) %collective-permute-start.4) | collective-permute-done | bytes 401440 | tf_op jit(solution)/shard_map/ppermute | solution.py:34
  156.1 12.3 %shard_map.91.refs_1_ = f32[784,128]{1,0:T(8,128)S(1)} custom-call(f32[784,128]{1,0:T(8,128)S(1)} %shard_map.89.mine, f32[784,128]{1,0:T(8,128)} %collective-permute-done.4.other), custom_call_target="tpu_custom_call" | custom-call | flops 1000000000 | bytes 1000000 | tf_op jit(solution)/shard_map/pallas_call | solution.py:457
  169.2 10.3 %shard_map.92 = f32[16,24,8,128]{3,2,1,0:T(8,128)S(1)} custom-call(f32[16,24,1152]{2,1,0:T(8,128)S(1)} %all-to-all-done.refs_0_, f32[784,128]{1,0:T(8,128)S(1)} %shard_map.91.refs_1_, s32[96]{0:T(128)S(1)} %copy-done.10), custom_call_target="tpu_custom_call" | custom-call | flops 1000000000 | bytes 4000000 | tf_op jit(solution)/shard_map/pallas_call | solution.py:457
  180.7 4.5 %all-to-all-start.2 = ((f32[16,24,8,128]{3,2,1,0:T(8,128)}), f32[16,24,8,128]{3,2,1,0:T(8,128)}, u32[]{:S(2)}, u32[]{:S(2)}) async-start(f32[16,24,8,128]{3,2,1,0:T(8,128)} %copy-done.3), calls=%async_computation.2 | async-start | bytes 3145728 | tf_op jit(solution)/shard_map/all_to_all | solution.py:496
  188.2 23.6 %collective-permute-done.5.refs_1_ = f32[784,128]{1,0:T(8,128)S(1)} collective-permute-done((f32[784,128]{1,0:T(8,128)S(1)}, f32[784,128]{1,0:T(8,128)S(1)}, u32[]{:S(2)}, u32[]{:S(2)}) %collective-permute-start.5) | collective-permute-done | bytes 401440 | tf_op jit(solution)/shard_map/ppermute | solution.py:34
  211.8 10.3 %shard_map.93 = f32[16,24,8,128]{3,2,1,0:T(8,128)S(1)} custom-call(f32[16,24,1152]{2,1,0:T(8,128)S(1)} %all_to_all.20.refs_0_, f32[784,128]{1,0:T(8,128)S(1)} %collective-permute-done.5.refs_1_, s32[96]{0:T(128)S(1)} %copy-done.10), custom_call_target="tpu_custom_call" | custom-call | flops 1000000000 | bytes 4000000 | tf_op jit(solution)/shard_map/pallas_call | solution.py:457
  222.2 30.3 %all_to_all.21.other = f32[16,24,8,128]{3,2,1,0:T(8,128)} all-to-all(f32[16,24,8,128]{3,2,1,0:T(8,128)S(1)} %shard_map.93), channel_id=1, replica_groups={{0,1,2,3,8,9,10,11,16,17,18,19,24,25,26,27},{4,5,6,7,12,13,14,15,20,21,..., dimensions={0} | all-to-all | bytes 3145728 | tf_op jit(solution)/shard_map/all_to_all | solution.py:496
  252.4 4.2 %shard_map.94 = f32[24,8,4096]{2,1,0:T(8,128)} custom-call(f32[16,24,8,128]{3,2,1,0:T(8,128)} %all-to-all-done.2.mine, f32[16,24,8,128]{3,2,1,0:T(8,128)} %all_to_all.21.other, s32[1]{0:T(128)} %bitcast.zh), custom_call_target="tpu_custom_call" | custom-call | tf_op jit(solution)/shard_map/pallas_call | solution.py:600
  (39 shorter events, 22.2 us)
Async XLA Ops:
  0.0 1.9 copy-start
  1.9 1.0 copy-start.1
  9.2 24.7 %collective-permute-start.2 = (f32[6,8,4096]{2,1,0:T(8,128)}, f32[6,8,4096]{2,1,0:T(8,128)}, u32[]{:S(2)}, u32[]{:S(2)}) collective-permute-start(f32[6,8,4096]{2,1,0:T(8,128)} %get-tuple-element.24), channel_id=1, source_target_pairs={{7,0},{0,1},{1,2},{2,3},{3,4},{4,5},{5,6},{6,7},{15,8},{8,9},{9,10... | collective-permute-start | bytes 2359304 | tf_op jit(solution)/shard_map/ppermute | solution.py:34
  18.6 1.0 copy-start.6
  19.5 14.4 %copy-start.2 = (f32[3,8,4096]{2,1,0:T(8,128)S(1)}, f32[3,8,4096]{2,1,0:T(8,128)}, u32[]{:S(2)}) copy-start(f32[3,8,4096]{2,1,0:T(8,128)} %ratios.11) | copy-start | bytes 1179652
  19.5 31.3 %collective-permute-start.1 = (f32[6,8,4096]{2,1,0:T(8,128)}, f32[6,8,4096]{2,1,0:T(8,128)}, u32[]{:S(2)}, u32[]{:S(2)}) collective-permute-start(f32[6,8,4096]{2,1,0:T(8,128)} %get-tuple-element.22), channel_id=1, source_target_pairs={{7,0},{0,1},{1,2},{2,3},{3,4},{4,5},{5,6},{6,7},{15,8},{8,9},{9,10... | collective-permute-start | bytes 2359304 | tf_op jit(solution)/shard_map/ppermute | solution.py:34
  27.4 1.0 copy-start.4
  28.4 22.4 %copy-start.7 = (f32[8,8,4096]{2,1,0:T(8,128)S(1)}, f32[8,8,4096]{2,1,0:T(8,128)}, u32[]{:S(2)}) copy-start(f32[8,8,4096]{2,1,0:T(8,128)} %copy-done.6) | copy-start | bytes 3145732
  28.4 38.4 %collective-permute-start = (f32[6,8,4096]{2,1,0:T(8,128)}, f32[6,8,4096]{2,1,0:T(8,128)}, u32[]{:S(2)}, u32[]{:S(2)}) collective-permute-start(f32[6,8,4096]{2,1,0:T(8,128)} %get-tuple-element.20), channel_id=1, source_target_pairs={{7,0},{0,1},{1,2},{2,3},{3,4},{4,5},{5,6},{6,7},{15,8},{8,9},{9,10... | collective-permute-start | bytes 2359304 | tf_op jit(solution)/shard_map/ppermute | solution.py:34
  50.8 16.0 %copy-start.5 = (f32[8,8,4096]{2,1,0:T(8,128)S(1)}, f32[8,8,4096]{2,1,0:T(8,128)}, u32[]{:S(2)}) copy-start(f32[8,8,4096]{2,1,0:T(8,128)} %copy-done.4) | copy-start | bytes 3145732
  102.1 7.2 %copy-start.11 = (s32[16]{0:T(128)S(1)}, s32[16]{0:T(128)}, u32[]{:S(2)}) copy-start(s32[16]{0:T(128)} %count.1) | copy-start | bytes 196
  102.1 36.1 %all-to-all-start = ((f32[16,24,1152]{2,1,0:T(8,128)}), f32[16,24,1152]{2,1,0:T(8,128)S(1)}, u32[]{:S(2)}, u32[]{:S(2)}) async-start(f32[16,24,1152]{2,1,0:T(8,128)} %get-tuple-element.29), calls=%async_computation | async-start | bytes 3538944 | tf_op jit(solution)/shard_map/all_to_all | solution.py:496
  113.3 0.7 copy-start.12
  114.0 14.9 %collective-permute-start.3 = (f32[16,8,256]{2,1,0:T(8,128)S(1)}, f32[16,8,256]{2,1,0:T(8,128)S(1)}, u32[]{:S(2)}, u32[]{:S(2)}) collective-permute-start(f32[16,8,256]{2,1,0:T(8,128)S(1)} %get-tuple-element.32), channel_id=1, source_target_pairs={{4,0},{5,1},{6,2},{7,3},{0,4},{1,5},{2,6},{3,7},{12,8},{13,9},{14,... | collective-permute-start | bytes 393224 | tf_op jit(solution)/shard_map/ppermute | solution.py:34
  134.7 21.4 %collective-permute-start.4 = (f32[784,128]{1,0:T(8,128)}, f32[784,128]{1,0:T(8,128)}, u32[]{:S(2)}, u32[]{:S(2)}) collective-permute-start(f32[784,128]{1,0:T(8,128)} %shard_map.90), channel_id=1, source_target_pairs={{4,0},{5,1},{6,2},{7,3},{0,4},{1,5},{2,6},{3,7},{12,8},{13,9},{14,... | collective-permute-start | bytes 1204232 | tf_op jit(solution)/shard_map/ppermute | solution.py:34
  138.1 0.9 copy-start.13
  144.1 25.2 %copy-start.10 = (s32[96]{0:T(128)S(1)}, s32[96]{0:T(128)}, u32[]{:S(2)}) copy-start(s32[96]{0:T(128)} %refs_2_.3) | copy-start | bytes 1156
  168.4 0.8 copy-start.8
  179.5 1.1 copy-start.3
  180.7 4.6 %copy-start.9 = (f32[784,128]{1,0:T(8,128)S(1)}, f32[784,128]{1,0:T(8,128)}, u32[]{:S(2)}) copy-start(f32[784,128]{1,0:T(8,128)} %copy-done.8) | copy-start | bytes 1204228
  180.7 41.5 %all-to-all-start.2 = ((f32[16,24,8,128]{3,2,1,0:T(8,128)}), f32[16,24,8,128]{3,2,1,0:T(8,128)}, u32[]{:S(2)}, u32[]{:S(2)}) async-start(f32[16,24,8,128]{3,2,1,0:T(8,128)} %copy-done.3), calls=%async_computation.2 | async-start | bytes 3145728 | tf_op jit(solution)/shard_map/all_to_all | solution.py:496
  185.3 26.6 %collective-permute-start.5 = (f32[784,128]{1,0:T(8,128)S(1)}, f32[784,128]{1,0:T(8,128)S(1)}, u32[]{:S(2)}, u32[]{:S(2)}) collective-permute-start(f32[784,128]{1,0:T(8,128)S(1)} %copy-done.9), channel_id=1, source_target_pairs={{4,0},{5,1},{6,2},{7,3},{0,4},{1,5},{2,6},{3,7},{12,8},{13,9},{14,... | collective-permute-start | bytes 1204232 | tf_op jit(solution)/shard_map/ppermute | solution.py:34
